TPU v7x, 512 devices: a whole 4x8x8 slice. The times are simulated.
512 devices in a mesh: wide: 32 (over z_lo, x, core), narrow: 16 (over z_hi, y).
Axes of the slice: x: 4, y: 8, z: 8 (z_hi: 2, z_lo: 4; z = z_hi * 4 + z_lo), core: 2. Of those that a mesh axis runs over, the one named last changes fastest.
Arguments:
- exposures: bfloat16 [4, 512, 12288], P(None, 'narrow', 'wide'), may hold values from -6 to 6
- basis_kernels: bfloat16 [5, 21, 21], replicated, may hold values from -0.25 to 0.25
- poly_coef: float32 [4, 5, 6], replicated, may hold values from -3 to 3
- exposure_weight: float32 [4], replicated, may hold values from 0.5 to 2
- row_start: int32 [4], replicated, may hold values from 0 to 256, as said below
- row_count: int32 [4], replicated, may hold values from 128 to 512, as said below
- filter_taps: float32 [21], replicated, may hold values from -1.5 to 1.5
Outputs:
- coadded: float32 [512, 12288], P('narrow', 'wide')
- detection: float32 [512, 12288], P('narrow', 'wide')
Inputs may be any that keep to these rules, and one draw needn't show every extreme that they name: Each row_start is a multiple of 32; row_start[0] is 0 and row_start + row_count never exceeds 512. Each row_count is a multiple of 8; exposure 0 covers the whole band.
All inputs are finite; a program needn't handle non-finite values.
Results may differ from a plain program's by a relative error of at most 0.0003.
Values may be sent and summed in bfloat16 or wider, within the bound.
A program may use at most 64 MiB of HBM per device.

v0:
```python
import math

import jax
import jax.numpy as jnp
from jax import lax
from jax.sharding import PartitionSpec as P


def padded(array, sides, width):
    for axis, dim in sides:
        peers, length = (lax.axis_size(axis), array.shape[dim])
        up = [(i, (i + 1) % peers) for i in range(peers - 1)]
        down = [(j, i) for i, j in up]
        last = lax.slice_in_dim(array, length - width, length, axis=dim)
        initial = lax.slice_in_dim(array, 0, width, axis=dim)
        before = lax.ppermute(last, axis, up)
        after = lax.ppermute(initial, axis, down)
        array = jnp.concatenate([before, array, after], axis=dim)
    return array


def respond(window, basis_kernels):
    side = basis_kernels.shape[1]
    kernel_total = basis_kernels.shape[0]
    out_rows = window.shape[0] - (side - 1)
    out_cols = window.shape[1] - (side - 1)
    block = math.gcd(out_cols, 128)
    block_total = out_cols // block
    span = block + side - 1
    shifted = jnp.stack([window[offset : offset + out_rows] for offset in range(side)])
    patches = jnp.stack(
        [shifted[:, :, index * block : index * block + span] for index in range(block_total)]
    )
    lagged = (
        jnp.arange(span, dtype=jnp.int32)[:, None] - jnp.arange(block, dtype=jnp.int32)[None, :]
    )
    onehot = (lagged[None] == jnp.arange(side, dtype=jnp.int32)[:, None, None]).astype(jnp.float32)
    table = jnp.einsum(
        "kab,bco->acko", basis_kernels.astype(jnp.float32), onehot, precision=lax.Precision.HIGHEST
    )
    table = table.astype(jnp.bfloat16).reshape(side, span, kernel_total * block)
    result = jnp.einsum("jarc,acn->jrn", patches, table, preferred_element_type=jnp.float32)
    result = result.reshape(block_total, out_rows, kernel_total, block).transpose(2, 1, 0, 3)
    return result.reshape(kernel_total, out_rows, out_cols)


def on_device(
    exposures, basis_kernels, poly_coef, exposure_weight, row_start, row_count, filter_taps
):
    tile_rows = exposures.shape[1]
    tile_cols = exposures.shape[2]
    band_rows = tile_rows * lax.axis_size("narrow")
    band_cols = tile_cols * lax.axis_size("wide")
    row_base = lax.axis_index("narrow") * tile_rows
    row_index = row_base + jnp.arange(tile_rows, dtype=jnp.int32)
    col_index = lax.axis_index("wide") * tile_cols + jnp.arange(tile_cols, dtype=jnp.int32)
    y_coord = ((2 * row_index + 1).astype(jnp.float32) / band_rows - 1.0)[:, None]
    x_coord = ((2 * col_index + 1).astype(jnp.float32) / band_cols - 1.0)[None, :]
    numerator = jnp.zeros((tile_rows, tile_cols), jnp.float32)
    denominator = jnp.zeros((tile_rows, 1), jnp.float32)
    zero_value = jnp.zeros((), exposures.dtype)
    for member in range(exposures.shape[0]):
        first_row = row_start[member]
        row_total = row_count[member]
        inside = (row_index >= first_row) & (row_index < first_row + row_total)
        lead_row = row_base - 10 - first_row

        def placed_rows(window, portion, anchor, lead_row=lead_row):
            window_len = window.shape[0]
            portion_len = portion.shape[0]
            padding = jnp.zeros((window_len, portion.shape[1]), portion.dtype)
            extended = jnp.concatenate([padding, portion, padding], 0)
            sliced = lax.dynamic_slice_in_dim(extended, lead_row + window_len, window_len, 0)
            local_rows = lead_row + jnp.arange(window_len, dtype=jnp.int32)
            present = (local_rows >= 0) & (local_rows < portion_len)
            return jnp.where(present[:, None], sliced, window)

        empty_window = jnp.zeros((tile_rows + 20, tile_cols), exposures.dtype)
        window = placed_rows(
            empty_window,
            lax.all_gather(exposures[member], "narrow", axis=0, tiled=True),
            jnp.int32(0),
        )
        window_rows = row_base - 10 + jnp.arange(tile_rows + 20, dtype=jnp.int32)
        valid_rows = (window_rows >= first_row) & (window_rows < first_row + row_total)
        window = jnp.where(valid_rows[:, None], window, zero_value)
        window = padded(window, (("wide", 1),), 10)
        touches = (first_row < row_base + tile_rows) & (first_row + row_total > row_base)

        def matched_tile(window, member=member):
            response = respond(window, basis_kernels)
            matched = jnp.zeros((tile_rows, tile_cols), jnp.float32)
            for kernel in range(basis_kernels.shape[0]):
                coeffs = poly_coef[member, kernel]
                spatial = (
                    coeffs[0]
                    + coeffs[1] * x_coord
                    + coeffs[2] * y_coord
                    + coeffs[3] * x_coord * x_coord
                    + coeffs[4] * x_coord * y_coord
                    + coeffs[5] * y_coord * y_coord
                )
                matched = matched + spatial * response[kernel]
            return matched

        def empty_tile(window):
            return jnp.zeros((tile_rows, tile_cols), jnp.float32)

        matched = lax.cond(touches, matched_tile, empty_tile, window)
        weighting = exposure_weight[member] * inside.astype(jnp.float32)[:, None]
        numerator = numerator + weighting * matched
        denominator = denominator + weighting
    coadded = numerator / denominator
    taps_total = filter_taps.shape[0]
    framed = padded(coadded, (("wide", 1),), 10)
    inner = filter_taps[0] * framed[:, 0:tile_cols]
    for offset in range(1, taps_total):
        inner = inner + filter_taps[offset] * framed[:, offset : offset + tile_cols]
    across = padded(inner, (("narrow", 0),), 10)
    detection = filter_taps[0] * across[0:tile_rows]
    for offset in range(1, taps_total):
        detection = detection + filter_taps[offset] * across[offset : offset + tile_rows]
    return (coadded, detection)


def solution(mesh):
    placed = (P(None, "narrow", "wide"), P(), P(), P(), P(), P(), P())
    return jax.shard_map(
        on_device,
        mesh=mesh,
        in_specs=placed,
        out_specs=(P("narrow", "wide"), P("narrow", "wide")),
        check_vma=False,
    )
```

profile of v0, /device:TPU:384, one launch (start us, length us, event | category | flops | bytes accessed | tf_op | source)
XLA Modules:
  0.0 495.4 jit_solution(2599510035167982765)
XLA Ops:
  6.4 50.4 %all-gather.3 = bf16[1,512,384]{2,1,0:T(8,128)(2,1)S(1)} all-gather(bf16[1,32,384]{2,1,0:T(8,128)(2,1)S(1)} %get-tuple-element.333), channel_id=5, replica_groups=mesh['wide'=32,'narrow'=16] {'narrow'}, dimensions={1}, use_global_device_ids=true | all-gather | bytes 417792 | tf_op jit(solution)/shard_map/all_gather | solution.py:81
  65.1 50.3 %all-gather = bf16[1,512,384]{2,1,0:T(8,128)(2,1)S(1)} all-gather(bf16[1,32,384]{2,1,0:T(8,128)(2,1)S(1)} %get-tuple-element.331), channel_id=2, replica_groups=mesh['wide'=32,'narrow'=16] {'narrow'}, dimensions={1}, use_global_device_ids=true | all-gather | bytes 417792 | tf_op jit(solution)/shard_map/all_gather | solution.py:81
  117.3 49.7 %all-gather.1 = bf16[1,512,384]{2,1,0:T(8,128)(2,1)S(1)} all-gather(bf16[1,32,384]{2,1,0:T(8,128)(2,1)S(1)} %get-tuple-element.332), channel_id=3, replica_groups=mesh['wide'=32,'narrow'=16] {'narrow'}, dimensions={1}, use_global_device_ids=true | all-gather | bytes 417792 | tf_op jit(solution)/shard_map/all_gather | solution.py:81
  168.3 49.0 %all-gather.2 = bf16[1,512,384]{2,1,0:T(8,128)(2,1)S(1)} all-gather(bf16[1,32,384]{2,1,0:T(8,128)(2,1)S(1)} %get-tuple-element.334), channel_id=4, replica_groups=mesh['wide'=32,'narrow'=16] {'narrow'}, dimensions={1}, use_global_device_ids=true | all-gather | bytes 417792 | tf_op jit(solution)/shard_map/all_gather | solution.py:81
  223.4 5.3 %collective-permute-start.3 = (bf16[52,10]{1,0:T(8,128)(2,1)S(1)}, bf16[52,10]{1,0:T(8,128)(2,1)S(1)}, u32[]{:S(2)}, u32[]{:S(2)}) collective-permute-start(bf16[52,10]{1,0:T(8,128)(2,1)S(1)} %get-tuple-element.345), channel_id=1, source_target_pairs={{16,0},{32,16},{48,32},{64,48},{80,64},{96,80},{112,96},{128,112},... | collective-permute-start | bytes 3128 | tf_op jit(solution)/shard_map/ppermute | solution.py:17
  230.1 5.0 %add_add_fusion = (f32[32]{0:T(128)S(1)}, f32[32]{0:T(128)S(1)}, f32[32]{0:T(128)S(1)}, f32[32]{0:T(128)S(1)}, f32[32]{0:T(128)S(1)}) fusion(f32[]{:T(128)} %bitcast.314, s32[]{:T(128)S(6)} %add.1350, s32[]{:T(128)} %bitcast.312, s32[]{:T(128)S(6)} %mul.1366, f32[]{:T(128)} %bitcast.310, s32[]{:T(128)S(6)} %add.1334, s32[]{:T(128)} %bitcast.308, ...), kind=kLoop, calls=%fused_computation.570 | loop fusion | flops 640 | bytes 692 | tf_op jit(solution)/shard_map/add | solution.py:112
  239.7 5.8 %collective-permute-start.1 = (bf16[52,10]{1,0:T(8,128)(2,1)S(1)}, bf16[52,10]{1,0:T(8,128)(2,1)S(1)}, u32[]{:S(2)}, u32[]{:S(2)}) collective-permute-start(bf16[52,10]{1,0:T(8,128)(2,1)S(1)} %get-tuple-element.340), channel_id=1, source_target_pairs={{16,0},{32,16},{48,32},{64,48},{80,64},{96,80},{112,96},{128,112},... | collective-permute-start | bytes 3128 | tf_op jit(solution)/shard_map/ppermute | solution.py:17
  247.7 5.0 %collective-permute-done = bf16[52,10]{1,0:T(8,128)(2,1)S(1)} collective-permute-done((bf16[52,10]{1,0:T(8,128)(2,1)S(1)}, bf16[52,10]{1,0:T(8,128)(2,1)S(1)}, u32[]{:S(2)}, u32[]{:S(2)}) %collective-permute-start) | collective-permute-done | bytes 1072 | tf_op jit(solution)/shard_map/ppermute | solution.py:16
  252.8 48.0 %conditional.7 = (f32[32,384]{1,0:T(8,128)S(1)}) conditional(s32[]{:T(128)} %convert_element_type.81, () %tuple.38, (f32[4,5,6]{2,0,1:T(4,128)S(1)}, f32[1,384]{1,0:T(1,128)S(1)}, f32[32,1]{0,1:T(1,128)S(1)}, bf16[52,404]{1,0:T(8,128)(2,1)S(1)}, bf16[5,21,21]{2,1,0:T(8,128)(2,1)S(1)}) %tuple.324), branch_computations={%region_6.7_spmd, %region_7.8_spmd} | conditional | flops 470078048 | bytes 36717480 | solution.py:109
  258.1 8.9 %reshape.485 = bf16[21,148,640]{2,1,0:T(8,128)(2,1)} reshape(bf16[21,148,5,128]{3,2,1,0:T(8,128)(2,1)} %copy.30) | data formatting | bytes 7956480 | tf_op jit(solution)/shard_map/cond/branch_1_fun/reshape | solution.py:41
  267.0 8.8 %dot_general.38 = bf16[5,128,21,148]{1,0,3,2:T(8,128)(2,1)} reshape(bf16[640,21,148]{0,2,1:T(8,128)(2,1)} %bitcast.689) | data formatting | bytes 7956480 | tf_op jit(solution)/shard_map/cond/branch_1_fun/jarc,acn->jrn/dot_general | solution.py:42
  281.8 6.2 %multiply_bitcast_fusion.19 = (f32[32]{0:T(128)S(1)}, f32[32]{0:T(128)S(1)}, f32[32]{0:T(128)S(1)}, f32[32]{0:T(128)S(1)}, f32[32]{0:T(128)S(1)}, /*index=5*/f32...) fusion(f32[32,1]{0,1:T(1,128)S(1)} %get-tuple-element.69, f32[]{:T(128)} %bitcast.233, ...), kind=kLoop, calls=%fused_computation.334 | loop fusion | flops 480 | bytes 1448 | tf_op jit(solution)/shard_map/cond/branch_1_fun/add | solution.py:96
  288.0 11.3 %add_reduce_fusion.19 = (f32[384]{0:T(512)S(1)}, f32[384]{0:T(512)S(1)}, f32[384]{0:T(512)S(1)}, f32[384]{0:T(512)S(1)}, f32[384]{0:T(512)S(1)}, /*index=5*/f32[...) fusion(f32[1,384]{1,0:T(1,128)S(1)} %get-tuple-element.68, ...), kind=kLoop, calls=%fused_computation.319 | loop fusion | flops 8448 | bytes 21576 | tf_op jit(solution)/shard_map/cond/branch_1_fun/add | solution.py:96
  300.8 48.2 %conditional.6 = (f32[32,384]{1,0:T(8,128)S(1)}) conditional(s32[]{:T(128)} %convert_element_type.80, () %tuple.36, (f32[4,5,6]{2,0,1:T(4,128)S(1)}, f32[1,384]{1,0:T(1,128)S(1)}, f32[32,1]{0,1:T(1,128)S(1)}, bf16[52,404]{1,0:T(8,128)(2,1)S(1)}, bf16[5,21,21]{2,1,0:T(8,128)(2,1)S(1)}) %tuple.325), branch_computations={%region_4.5_spmd, %region_5.6_spmd} | conditional | flops 470078048 | bytes 36717480 | solution.py:109
  306.3 8.9 %reshape.484 = bf16[21,148,640]{2,1,0:T(8,128)(2,1)} reshape(bf16[21,148,5,128]{3,2,1,0:T(8,128)(2,1)} %copy.23) | data formatting | bytes 7956480 | tf_op jit(solution)/shard_map/cond/branch_1_fun/reshape | solution.py:41
  315.2 8.8 %dot_general.34 = bf16[5,128,21,148]{1,0,3,2:T(8,128)(2,1)} reshape(bf16[640,21,148]{0,2,1:T(8,128)(2,1)} %bitcast.690) | data formatting | bytes 7956480 | tf_op jit(solution)/shard_map/cond/branch_1_fun/jarc,acn->jrn/dot_general | solution.py:42
  330.0 6.3 %multiply_bitcast_fusion.14 = (f32[32]{0:T(128)S(1)}, f32[32]{0:T(128)S(1)}, f32[32]{0:T(128)S(1)}, f32[32]{0:T(128)S(1)}, f32[32]{0:T(128)S(1)}, /*index=5*/f32...) fusion(f32[32,1]{0,1:T(1,128)S(1)} %get-tuple-element.64, f32[]{:T(128)} %bitcast.156, ...), kind=kLoop, calls=%fused_computation.250 | loop fusion | flops 480 | bytes 1448 | tf_op jit(solution)/shard_map/cond/branch_1_fun/add | solution.py:96
  336.3 11.3 %add_reduce_fusion.14 = (f32[384]{0:T(512)S(1)}, f32[384]{0:T(512)S(1)}, f32[384]{0:T(512)S(1)}, f32[384]{0:T(512)S(1)}, f32[384]{0:T(512)S(1)}, /*index=5*/f32[...) fusion(f32[1,384]{1,0:T(1,128)S(1)} %get-tuple-element.63, ...), kind=kLoop, calls=%fused_computation.235 | loop fusion | flops 8448 | bytes 21576 | tf_op jit(solution)/shard_map/cond/branch_1_fun/add | solution.py:96
  349.0 48.2 %conditional.5 = (f32[32,384]{1,0:T(8,128)S(1)}) conditional(s32[]{:T(128)} %convert_element_type.79, () %tuple.34, (f32[4,5,6]{2,0,1:T(4,128)S(1)}, f32[1,384]{1,0:T(1,128)S(1)}, f32[32,1]{0,1:T(1,128)S(1)}, bf16[52,404]{1,0:T(8,128)(2,1)S(1)}, bf16[5,21,21]{2,1,0:T(8,128)(2,1)S(1)}) %tuple.326), branch_computations={%region_2.3_spmd, %region_3.4_spmd} | conditional | flops 470078048 | bytes 36717480 | solution.py:109
  354.5 8.9 %reshape.483 = bf16[21,148,640]{2,1,0:T(8,128)(2,1)} reshape(bf16[21,148,5,128]{3,2,1,0:T(8,128)(2,1)} %copy.16) | data formatting | bytes 7956480 | tf_op jit(solution)/shard_map/cond/branch_1_fun/reshape | solution.py:41
  363.4 8.8 %dot_general.26 = bf16[5,128,21,148]{1,0,3,2:T(8,128)(2,1)} reshape(bf16[640,21,148]{0,2,1:T(8,128)(2,1)} %bitcast.691) | data formatting | bytes 7956480 | tf_op jit(solution)/shard_map/cond/branch_1_fun/jarc,acn->jrn/dot_general | solution.py:42
  378.2 6.2 %multiply_bitcast_fusion.9 = (f32[32]{0:T(128)S(1)}, f32[32]{0:T(128)S(1)}, f32[32]{0:T(128)S(1)}, f32[32]{0:T(128)S(1)}, f32[32]{0:T(128)S(1)}, /*index=5*/f32[...) fusion(f32[32,1]{0,1:T(1,128)S(1)} %get-tuple-element.59, f32[]{:T(128)} %bitcast.79, ...), kind=kLoop, calls=%fused_computation.166 | loop fusion | flops 480 | bytes 1448 | tf_op jit(solution)/shard_map/cond/branch_1_fun/add | solution.py:96
  384.5 11.2 %add_reduce_fusion.9 = (f32[384]{0:T(512)S(1)}, f32[384]{0:T(512)S(1)}, f32[384]{0:T(512)S(1)}, f32[384]{0:T(512)S(1)}, f32[384]{0:T(512)S(1)}, /*index=5*/f32[3...) fusion(f32[1,384]{1,0:T(1,128)S(1)} %get-tuple-element.58, ...), kind=kLoop, calls=%fused_computation.151 | loop fusion | flops 8448 | bytes 21576 | tf_op jit(solution)/shard_map/cond/branch_1_fun/add | solution.py:96
  397.2 48.2 %conditional.4 = (f32[32,384]{1,0:T(8,128)S(1)}) conditional(s32[]{:T(128)} %convert_element_type.76, () %tuple.32, (f32[4,5,6]{2,0,1:T(4,128)S(1)}, f32[1,384]{1,0:T(1,128)S(1)}, f32[32,1]{0,1:T(1,128)S(1)}, bf16[52,404]{1,0:T(8,128)(2,1)S(1)}, bf16[5,21,21]{2,1,0:T(8,128)(2,1)S(1)}) %tuple.327), branch_computations={%region_0.1_spmd, %region_1.2_spmd} | conditional | flops 470078048 | bytes 36717480 | solution.py:109
  402.7 8.9 %reshape.482 = bf16[21,148,640]{2,1,0:T(8,128)(2,1)} reshape(bf16[21,148,5,128]{3,2,1,0:T(8,128)(2,1)} %copy.9) | data formatting | bytes 7956480 | tf_op jit(solution)/shard_map/cond/branch_1_fun/reshape | solution.py:41
  411.6 8.8 %dot_general.18 = bf16[5,128,21,148]{1,0,3,2:T(8,128)(2,1)} reshape(bf16[640,21,148]{0,2,1:T(8,128)(2,1)} %bitcast.692) | data formatting | bytes 7956480 | tf_op jit(solution)/shard_map/cond/branch_1_fun/jarc,acn->jrn/dot_general | solution.py:42
  426.4 6.2 %multiply_bitcast_fusion.4 = (f32[32]{0:T(128)S(1)}, f32[32]{0:T(128)S(1)}, f32[32]{0:T(128)S(1)}, f32[32]{0:T(128)S(1)}, f32[32]{0:T(128)S(1)}, /*index=5*/f32[...) fusion(f32[32,1]{0,1:T(1,128)S(1)} %get-tuple-element.48, f32[]{:T(128)} %bitcast.2, ...), kind=kLoop, calls=%fused_computation.82 | loop fusion | flops 480 | bytes 1448 | tf_op jit(solution)/shard_map/cond/branch_1_fun/add | solution.py:96
  432.7 11.2 %add_reduce_fusion.4 = (f32[384]{0:T(512)S(1)}, f32[384]{0:T(512)S(1)}, f32[384]{0:T(512)S(1)}, f32[384]{0:T(512)S(1)}, f32[384]{0:T(512)S(1)}, /*index=5*/f32[3...) fusion(f32[1,384]{1,0:T(1,128)S(1)} %get-tuple-element.47, ...), kind=kLoop, calls=%fused_computation.67 | loop fusion | flops 8448 | bytes 21576 | tf_op jit(solution)/shard_map/cond/branch_1_fun/add | solution.py:96
  450.6 4.1 collective-permute-done.8
  454.7 13.3 %fusion.119 = f32[32,384]{1,0:T(8,128)S(1)} fusion(f32[32,384]{1,0:T(8,128)S(1)} %add_divide_fusion, f32[32,10]{1,0:T(8,128)S(1)} %collective-permute-done.9, f32[32,10]{1,0:T(8,128)S(1)} %collective-permute-done.8, f32[]{:T(128)} %bitcast.344, f32[]{:T(128)} %bitcast.343, f32[]{:T(128)} %bitcast.342, f32[]{:T(128)} %bitcast.341, f32[]{:T(128)} %bitcast.340, ...), kind=kLoop, calls=%fused_computation.427 | loop fusion | flops 749568 | bytes 100948 | tf_op jit(solution)/shard_map/add | solution.py:118
  473.9 7.8 %collective-permute-done.10 = f32[10,384]{1,0:T(8,128)S(1)} collective-permute-done((f32[10,384]{1,0:T(8,128)S(1)}, f32[10,384]{1,0:T(8,128)S(1)}, u32[]{:S(2)}, u32[]{:S(2)}) %collective-permute-start.10) | collective-permute-done | bytes 15392 | tf_op jit(solution)/shard_map/ppermute | solution.py:16
  481.7 13.7 %fusion.175 = f32[32,384]{1,0:T(8,128)} fusion(f32[32,384]{1,0:T(8,128)S(1)} %fusion.119, f32[10,384]{1,0:T(8,128)S(1)} %collective-permute-done.11, f32[10,384]{1,0:T(8,128)S(1)} %collective-permute-done.10, f32[]{:T(128)} %bitcast.344, f32[]{:T(128)} %bitcast.343, f32[]{:T(128)} %bitcast.342, f32[]{:T(128)} %bitcast.341, f32[]{:T(128)} %bitcast.340, ...), kind=kLoop, calls=%fused_computation.483 | loop fusion | flops 749568 | bytes 129108 | tf_op jit(solution)/shard_map/add | solution.py:122
  (199 shorter events, 82.5 us)
Async XLA Ops:
  0.6 228.1 %copy-start.4 = (f32[4]{0:T(128)S(1)}, f32[4]{0:T(128)}, u32[]{:S(2)}) copy-start(f32[4]{0:T(128)} %param.18) | copy-start | bytes 52
  0.6 228.8 %copy-start.3 = (f32[21]{0:T(128)S(1)}, f32[21]{0:T(128)}, u32[]{:S(2)}) copy-start(f32[21]{0:T(128)} %param.21) | copy-start | bytes 256
  0.7 252.2 %copy-start.1 = (f32[4,5,6]{2,0,1:T(4,128)S(1)}, f32[4,5,6]{2,0,1:T(4,128)}, u32[]{:S(2)}) copy-start(f32[4,5,6]{2,0,1:T(4,128)} %param.17) | copy-start | bytes 1444
  0.7 252.2 %copy-start = (bf16[5,21,21]{2,1,0:T(8,128)(2,1)S(1)}, bf16[5,21,21]{2,1,0:T(8,128)(2,1)}, u32[]{:S(2)}) copy-start(bf16[5,21,21]{2,1,0:T(8,128)(2,1)} %param.16) | copy-start | bytes 13234
  57.7 180.0 %collective-permute-start.7 = (bf16[52,10]{1,0:T(8,128)(2,1)S(1)}, bf16[52,10]{1,0:T(8,128)(2,1)S(1)}, u32[]{:S(2)}, u32[]{:S(2)}) collective-permute-start(bf16[52,10]{1,0:T(8,128)(2,1)S(1)} %get-tuple-element.349), channel_id=1, source_target_pairs={{16,0},{32,16},{48,32},{64,48},{80,64},{96,80},{112,96},{128,112},... | collective-permute-start | bytes 3128 | tf_op jit(solution)/shard_map/ppermute | solution.py:17
  59.7 180.0 %collective-permute-start.6 = (bf16[52,10]{1,0:T(8,128)(2,1)S(1)}, bf16[52,10]{1,0:T(8,128)(2,1)S(1)}, u32[]{:S(2)}, u32[]{:S(2)}) collective-permute-start(bf16[52,10]{1,0:T(8,128)(2,1)S(1)} %get-tuple-element.348), channel_id=1, source_target_pairs={{0,16},{16,32},{32,48},{48,64},{64,80},{80,96},{96,112},{112,128},... | collective-permute-start | bytes 3128 | tf_op jit(solution)/shard_map/ppermute | solution.py:16
  219.0 26.6 %collective-permute-start.5 = (bf16[52,10]{1,0:T(8,128)(2,1)S(1)}, bf16[52,10]{1,0:T(8,128)(2,1)S(1)}, u32[]{:S(2)}, u32[]{:S(2)}) collective-permute-start(bf16[52,10]{1,0:T(8,128)(2,1)S(1)} %get-tuple-element.347), channel_id=1, source_target_pairs={{16,0},{32,16},{48,32},{64,48},{80,64},{96,80},{112,96},{128,112},... | collective-permute-start | bytes 3128 | tf_op jit(solution)/shard_map/ppermute | solution.py:17
  220.9 26.6 %collective-permute-start.4 = (bf16[52,10]{1,0:T(8,128)(2,1)S(1)}, bf16[52,10]{1,0:T(8,128)(2,1)S(1)}, u32[]{:S(2)}, u32[]{:S(2)}) collective-permute-start(bf16[52,10]{1,0:T(8,128)(2,1)S(1)} %get-tuple-element.346), channel_id=1, source_target_pairs={{0,16},{16,32},{32,48},{48,64},{64,80},{80,96},{96,112},{112,128},... | collective-permute-start | bytes 3128 | tf_op jit(solution)/shard_map/ppermute | solution.py:16
  223.4 24.2 %collective-permute-start.3 = (bf16[52,10]{1,0:T(8,128)(2,1)S(1)}, bf16[52,10]{1,0:T(8,128)(2,1)S(1)}, u32[]{:S(2)}, u32[]{:S(2)}) collective-permute-start(bf16[52,10]{1,0:T(8,128)(2,1)S(1)} %get-tuple-element.345), channel_id=1, source_target_pairs={{16,0},{32,16},{48,32},{64,48},{80,64},{96,80},{112,96},{128,112},... | collective-permute-start | bytes 3128 | tf_op jit(solution)/shard_map/ppermute | solution.py:17
  237.8 9.9 %collective-permute-start.2 = (bf16[52,10]{1,0:T(8,128)(2,1)S(1)}, bf16[52,10]{1,0:T(8,128)(2,1)S(1)}, u32[]{:S(2)}, u32[]{:S(2)}) collective-permute-start(bf16[52,10]{1,0:T(8,128)(2,1)S(1)} %get-tuple-element.344), channel_id=1, source_target_pairs={{0,16},{16,32},{32,48},{48,64},{64,80},{80,96},{96,112},{112,128},... | collective-permute-start | bytes 3128 | tf_op jit(solution)/shard_map/ppermute | solution.py:16
  239.7 8.0 %collective-permute-start.1 = (bf16[52,10]{1,0:T(8,128)(2,1)S(1)}, bf16[52,10]{1,0:T(8,128)(2,1)S(1)}, u32[]{:S(2)}, u32[]{:S(2)}) collective-permute-start(bf16[52,10]{1,0:T(8,128)(2,1)S(1)} %get-tuple-element.340), channel_id=1, source_target_pairs={{16,0},{32,16},{48,32},{64,48},{80,64},{96,80},{112,96},{128,112},... | collective-permute-start | bytes 3128 | tf_op jit(solution)/shard_map/ppermute | solution.py:17
  245.6 7.1 %collective-permute-start = (bf16[52,10]{1,0:T(8,128)(2,1)S(1)}, bf16[52,10]{1,0:T(8,128)(2,1)S(1)}, u32[]{:S(2)}, u32[]{:S(2)}) collective-permute-start(bf16[52,10]{1,0:T(8,128)(2,1)S(1)} %get-tuple-element.339), channel_id=1, source_target_pairs={{0,16},{16,32},{32,48},{48,64},{64,80},{80,96},{96,112},{112,128},... | collective-permute-start | bytes 3128 | tf_op jit(solution)/shard_map/ppermute | solution.py:16
  445.5 49.9 %copy-start.2 = (f32[32,384]{1,0:T(8,128)}, f32[32,384]{1,0:T(8,128)S(1)}, u32[]{:S(2)}) copy-start(f32[32,384]{1,0:T(8,128)S(1)} %add_divide_fusion) | copy-start | bytes 147460
  445.6 5.0 %collective-permute-start.9 = (f32[32,10]{1,0:T(8,128)S(1)}, f32[32,10]{1,0:T(8,128)S(1)}, u32[]{:S(2)}, u32[]{:S(2)}) collective-permute-start(f32[32,10]{1,0:T(8,128)S(1)} %get-tuple-element.338), channel_id=1, source_target_pairs={{16,0},{32,16},{48,32},{64,48},{80,64},{96,80},{112,96},{128,112},... | collective-permute-start | bytes 3848 | tf_op jit(solution)/shard_map/ppermute | solution.py:17
  447.5 7.2 %collective-permute-start.8 = (f32[32,10]{1,0:T(8,128)S(1)}, f32[32,10]{1,0:T(8,128)S(1)}, u32[]{:S(2)}, u32[]{:S(2)}) collective-permute-start(f32[32,10]{1,0:T(8,128)S(1)} %get-tuple-element.337), channel_id=1, source_target_pairs={{0,16},{16,32},{32,48},{48,64},{64,80},{80,96},{96,112},{112,128},... | collective-permute-start | bytes 3848 | tf_op jit(solution)/shard_map/ppermute | solution.py:16
  468.0 5.9 %collective-permute-start.11 = (f32[10,384]{1,0:T(8,128)S(1)}, f32[10,384]{1,0:T(8,128)S(1)}, u32[]{:S(2)}, u32[]{:S(2)}) collective-permute-start(f32[10,384]{1,0:T(8,128)S(1)} %get-tuple-element.336), channel_id=1, source_target_pairs={{1,0},{2,1},{3,2},{4,3},{5,4},{6,5},{7,6},{8,7},{9,8},{10,9},{11,1... | collective-permute-start | bytes 46088 | tf_op jit(solution)/shard_map/ppermute | solution.py:17
  469.9 11.7 %collective-permute-start.10 = (f32[10,384]{1,0:T(8,128)S(1)}, f32[10,384]{1,0:T(8,128)S(1)}, u32[]{:S(2)}, u32[]{:S(2)}) collective-permute-start(f32[10,384]{1,0:T(8,128)S(1)} %get-tuple-element.335), channel_id=1, source_target_pairs={{0,1},{1,2},{2,3},{3,4},{4,5},{5,6},{6,7},{7,8},{8,9},{9,10},{10,1... | collective-permute-start | bytes 46088 | tf_op jit(solution)/shard_map/ppermute | solution.py:16
where the time goes:
time: 499 us; the launch traced here: 495 us
  blocking collectives  199 us (40%)
  other arithmetic  111 us (22%)
  local copies, waits for them, and re-layouts  100 us (20%)
  starting transfers between devices  33.6 us (7%)
  matrix products  20.7 us (4%)
  waiting for transfers between devices  16.9 us (3%)
  between operations  11.2 us (2%)
    all_gather x4, blocking collectives, on_device(): lax.all_gather(exposures[member], 'narrow', axis=0, tiled=True)  199 us
    add x8, other arithmetic, matched_tile(): coeffs[0] + coeffs[1] * x_coord + coeffs[2] * y_coord  69.9 us
    reshape x4, local copies, waits for them, and re-layouts, respond(): table = table.astype(jnp.bfloat16).reshape(side, span, kernel_total * block)  35.6 us
    dot_general x4, local copies, waits for them, and re-layouts, respond(): jnp.einsum('jarc,acn->jrn', patches, table, preferred_element_type=jnp.fl...  35.1 us
    ppermute x6, starting transfers between devices, padded(): after = lax.ppermute(initial, axis, down)  18.7 us
    ppermute x6, waiting for transfers between devices, padded(): before = lax.ppermute(last, axis, up)  16.9 us
    convert_element_type x4, local copies, waits for them, and re-layouts, respond(): table = table.astype(jnp.bfloat16).reshape(side, span, kernel_total * block)  15.6 us
    dot_general x4, matrix products, respond(): jnp.einsum('jarc,acn->jrn', patches, table, preferred_element_type=jnp.fl...  15.4 us
  transfers between devices with their start and end apart: 12, of which 3 were waited for; matrix products, arithmetic and copies ran while one was open for 2% of the time, Pallas kernels for 0%

commit v1 on v0

v1 whole, which is shorter than its diff:
```python
import functools

import jax
import jax.numpy as jnp
from jax import lax
from jax.experimental import pallas as pl
from jax.experimental.pallas import tpu as pltpu
from jax.sharding import PartitionSpec as P

LANES = 128
SUBLANES = 8


def moved(array, shift):
    peers = lax.axis_size("narrow")
    if shift == 0:
        return array
    return lax.ppermute(array, "narrow", [(i, i + shift) for i in range(peers - shift)])


def placed_tiles(tiles, shifts, radix):
    for scale, digits in (
        (radix, [shift // radix for shift in shifts]),
        (1, [shift % radix for shift in shifts]),
    ):
        choice = digits[0]
        for digit in digits[1:]:
            choice = choice * radix + digit

        def branch(index, scale=scale):
            own = []
            for _ in tiles:
                own.append(index % radix)
                index //= radix
            own = own[::-1]

            def run(*operands):
                return tuple(moved(op, scale * step) for op, step in zip(operands, own))

            return run

        tiles = lax.switch(choice, [branch(i) for i in range(radix ** len(tiles))], *tiles)
    return tiles


def padded(array, axis, dim, width):
    peers, length = lax.axis_size(axis), array.shape[dim]
    up = [(i, i + 1) for i in range(peers - 1)]
    down = [(j, i) for i, j in up]
    before = lax.ppermute(lax.slice_in_dim(array, length - width, length, axis=dim), axis, up)
    after = lax.ppermute(lax.slice_in_dim(array, 0, width, axis=dim), axis, down)
    return jnp.concatenate([before, array, after], axis=dim)


def coadd_kernel(
    sizes,
    poly_ref,
    weight_ref,
    start_ref,
    count_ref,
    taps_ref,
    window_ref,
    seed_ref,
    coadd_ref,
    detect_ref,
    table,
    shifted,
    lhs,
    sums,
    spread,
):
    members, kernels, side, band_rows, band_cols, tile_rows, tile_cols = sizes
    half = side // 2
    step = LANES - (side - 1)
    blocks = pl.cdiv(tile_cols + 2 * half, step)
    rows = pl.cdiv(tile_rows + 2 * half, SUBLANES) * SUBLANES
    row_base = lax.axis_index("narrow") * tile_rows
    col_base = lax.axis_index("wide") * tile_cols

    for a in range(side):
        for k in range(kernels):
            seed = jnp.broadcast_to(seed_ref[k * side + a : k * side + a + 1, :], (LANES, LANES))
            band = pltpu.roll(seed, 0, 1, stride=1, stride_axis=0)
            table[a * LANES : (a + 1) * LANES, k * LANES : (k + 1) * LANES] = band.astype(
                jnp.bfloat16
            )

    all_rows = shifted.shape[1]
    window_rows = (
        row_base - 2 * half + lax.broadcasted_iota(jnp.int32, (all_rows, LANES), 0)
    )
    lane_in = lax.broadcasted_iota(jnp.int32, (all_rows, LANES), 1)
    out_row = row_base - half + lax.broadcasted_iota(jnp.int32, (rows, LANES), 0)
    y = (2 * out_row + 1).astype(jnp.float32) / band_rows - 1.0
    lane = lax.broadcasted_iota(jnp.int32, (rows, LANES), 1)
    cols = [col_base - half + block * step + lane for block in range(blocks)]
    denominator = jnp.zeros((rows, LANES), jnp.float32)
    sums[...] = jnp.zeros_like(sums)

    for e in range(members):
        first, total = start_ref[e], count_ref[e]
        inside = (out_row >= first) & (out_row < first + total)
        weighting = weight_ref[e] * inside.astype(jnp.float32)
        denominator = denominator + weighting
        touches = (first < row_base + tile_rows + half) & (first + total > row_base - half)

        @pl.when(touches)
        def _(e=e, first=first, total=total, weighting=weighting):
            valid = (window_rows >= first) & (window_rows < first + total)
            parts = []
            for tile in range(window_ref.shape[2] // LANES):
                part = window_ref[e, :, tile * LANES : (tile + 1) * LANES].astype(jnp.float32)
                parts.append(jnp.where(valid, part, 0.0))
            for block in range(blocks):
                tile, offset = divmod(block * step, LANES)
                here = parts[tile]
                if offset:
                    here = pltpu.roll(here, LANES - offset, 1)
                    if tile + 1 < len(parts):
                        after = pltpu.roll(parts[tile + 1], LANES - offset, 1)
                    else:
                        after = jnp.zeros_like(here)
                    here = jnp.where(lane_in < LANES - offset, here, after)
                shifted[block] = here
            for a in range(side):
                piece = jnp.concatenate(
                    [shifted[block, a : a + rows, :] for block in range(blocks)], axis=0
                )
                lhs[:, a * LANES : (a + 1) * LANES] = piece.astype(jnp.bfloat16)
            response = jnp.dot(lhs[...], table[...], preferred_element_type=jnp.float32)
            for block in range(blocks):
                x = (2 * cols[block] + 1).astype(jnp.float32) / band_cols - 1.0
                matched = jnp.zeros((rows, LANES), jnp.float32)
                for k in range(kernels):
                    p = [poly_ref[(e * kernels + k) * 6 + i] for i in range(6)]
                    spatial = (p[0] + y * (p[2] + p[5] * y)) + x * ((p[1] + p[4] * y) + p[3] * x)
                    matched = matched + spatial * response[
                        block * rows : (block + 1) * rows, k * LANES : (k + 1) * LANES
                    ]
                sums[block] += weighting * matched

    in_rows = (out_row >= 0) & (out_row < band_rows)
    divisor = jnp.where(in_rows, denominator, 1.0)
    coadds = []
    for block in range(blocks):
        keep = in_rows & (cols[block] >= 0) & (cols[block] < band_cols)
        coadds.append(jnp.where(keep, sums[block] / divisor, 0.0))
    tiles = spread.shape[1] // LANES
    for tile in range(tiles):
        line = jnp.zeros((rows, LANES), jnp.float32)
        for block in range(blocks):
            low = block * step - tile * LANES
            if low + step <= 0 or low >= LANES:
                continue
            turned = pltpu.roll(coadds[block], low % LANES, 1) if low % LANES else coadds[block]
            line = jnp.where((lane >= low) & (lane < low + step), turned, line)
        spread[:, tile * LANES : (tile + 1) * LANES] = line

    def ahead(parts, tile, offset):
        if offset == 0:
            return parts[tile]
        lanes = lax.broadcasted_iota(jnp.int32, parts[tile].shape, 1)
        here = pltpu.roll(parts[tile], LANES - offset, 1)
        after = pltpu.roll(parts[tile + 1], LANES - offset, 1)
        return jnp.where(lanes < LANES - offset, here, after)

    out_tiles = tile_cols // LANES
    own = [
        spread[half : half + tile_rows, i * LANES : (i + 1) * LANES] for i in range(tiles)
    ]
    for i in range(out_tiles):
        coadd_ref[:, i * LANES : (i + 1) * LANES] = ahead(own, i, half)
    down = []
    for i in range(tiles):
        total = taps_ref[0] * spread[0:tile_rows, i * LANES : (i + 1) * LANES]
        for t in range(1, side):
            total = total + taps_ref[t] * spread[
                t : t + tile_rows, i * LANES : (i + 1) * LANES
            ]
        down.append(total)
    for i in range(out_tiles):
        total = taps_ref[0] * ahead(down, i, 0)
        for t in range(1, side):
            total = total + taps_ref[t] * ahead(down, i, t)
        detect_ref[:, i * LANES : (i + 1) * LANES] = total


def on_device(
    exposures, basis_kernels, poly_coef, exposure_weight, row_start, row_count, filter_taps
):
    members, tile_rows, tile_cols = exposures.shape
    kernels, side = basis_kernels.shape[:2]
    half = side // 2
    band_rows = tile_rows * lax.axis_size("narrow")
    band_cols = tile_cols * lax.axis_size("wide")
    step = LANES - (side - 1)
    blocks = pl.cdiv(tile_cols + 2 * half, step)
    rows = pl.cdiv(tile_rows + 2 * half, SUBLANES) * SUBLANES
    all_rows = pl.cdiv(rows + side - 1, 2 * SUBLANES) * 2 * SUBLANES

    shifts = [row_start[e] // tile_rows for e in range(1, members)]
    tiles = placed_tiles(tuple(exposures[e] for e in range(1, members)), shifts, 3)
    window = jnp.stack([exposures[0], *tiles])
    window = padded(window, "narrow", 1, 2 * half)
    window = padded(window, "wide", 2, 2 * half)
    width = pl.cdiv(tile_cols + 4 * half, LANES) * LANES
    window = jnp.pad(
        window, ((0, 0), (0, all_rows - window.shape[1]), (0, width - window.shape[2]))
    )
    taps = basis_kernels.astype(jnp.float32).reshape(kernels * side, side)
    seed = jnp.concatenate(
        [taps[:, :1], jnp.zeros((kernels * side, step - 1), jnp.float32), taps[:, :0:-1]], axis=1
    )
    sizes = (members, kernels, side, band_rows, band_cols, tile_rows, tile_cols)
    out = jax.ShapeDtypeStruct((tile_rows, tile_cols), jnp.float32)
    scalars = pl.BlockSpec(memory_space=pltpu.SMEM)
    return pl.pallas_call(
        functools.partial(coadd_kernel, sizes),
        out_shape=(out, out),
        in_specs=[scalars] * 5 + [pl.BlockSpec(memory_space=pltpu.VMEM)] * 2,
        out_specs=(pl.BlockSpec(memory_space=pltpu.VMEM),) * 2,
        scratch_shapes=[
            pltpu.VMEM((side * LANES, kernels * LANES), jnp.bfloat16),
            pltpu.VMEM((blocks, all_rows, LANES), jnp.float32),
            pltpu.VMEM((blocks * rows, side * LANES), jnp.bfloat16),
            pltpu.VMEM((blocks, rows, LANES), jnp.float32),
            pltpu.VMEM((rows, width), jnp.float32),
        ],
        name="coadd",
    )(
        poly_coef.reshape(-1),
        exposure_weight,
        row_start,
        row_count,
        filter_taps,
        window,
        seed,
    )


def solution(mesh):
    placed = (P(None, "narrow", "wide"), P(), P(), P(), P(), P(), P())
    return jax.shard_map(
        on_device,
        mesh=mesh,
        in_specs=placed,
        out_specs=(P("narrow", "wide"), P("narrow", "wide")),
        check_vma=False,
    )
```

time: 499 us -> 87.7 us (0.18)
  the two profiles are of different devices: /device:TPU:384 before, /device:TPU:57 now
where the time goes in v1:
time: 87.7 us; the launch traced here: 86 us
  starting transfers between devices  45 us (51%)
  waiting for transfers between devices  19.6 us (22%)
  between operations  8.53 us (10%)
  Pallas kernels  8.5 us (10%)
  local copies, waits for them, and re-layouts  3.1 us (4%)
  other arithmetic  1.06 us (1%)
    ppermute x5, starting transfers between devices, moved(): lax.ppermute(array, 'narrow', [(i, i + shift) for i in range(peers - shif...  25.5 us
    ppermute x2, starting transfers between devices, padded(): lax.ppermute(lax.slice_in_dim(array, length - width, length, axis=dim), a...  15.7 us
    ppermute x2, waiting for transfers between devices, padded(): lax.ppermute(lax.slice_in_dim(array, 0, width, axis=dim), axis, down)  12.1 us
    pallas_call x1, Pallas kernels, on_device(): pl.pallas_call(functools.partial(coadd_kernel, sizes), out_shape=(out, ou...  8.5 us
    ppermute x5, waiting for transfers between devices, moved(): lax.ppermute(array, 'narrow', [(i, i + shift) for i in range(peers - shif...  7.54 us
    ppermute x2, starting transfers between devices, padded(): lax.ppermute(lax.slice_in_dim(array, 0, width, axis=dim), axis, down)  3.84 us
  transfers between devices with their start and end apart: 9, of which 5 were waited for; matrix products, arithmetic and copies ran while one was open for 2% of the time, Pallas kernels for 0%

profile of v1, /device:TPU:57, one launch (start us, length us, event | category | flops | bytes accessed | tf_op | source)
XLA Modules:
  0.0 86.0 jit_solution(17349865112192228732)
XLA Ops:
  0.6 1.4 %fusion.2 = (s32[1]{0:T(128)}, s32[1]{0:T(128)}, s32[1]{0:T(128)}) fusion(s32[4]{0:T(128)} %start_ref.1), kind=kLoop, calls=%fused_computation.14 | loop fusion | bytes 24 | tf_op jit(solution)/shard_map/slice | solution.py:201
  9.8 21.0 %conditional.2 = ((bf16[32,384]{1,0:T(8,128)(2,1)S(1)}, bf16[32,384]{1,0:T(8,128)(2,1)S(1)}, bf16[32,384]{1,0:T(8,128)(2,1)S(1)})) conditional(s32[]{:T(128)} %clamp.7, (bf16[32,384]{1,0:T(8,128)(2,1)S(1)}, bf16[32,384]{1,0:T(8,128)(2,1)S(1)}, bf16[32,384]{1,0:T(8,128)(2,1)S(1)}) %tuple.424, ...), branch_computations={%region_0.1_spmd, %region_1.2_spmd, %region_2.3_spmd, %region_3.4_... | conditional | bytes 442520 | solution.py:42
  9.9 12.2 %collective-permute-start.51 = (bf16[32,384]{1,0:T(8,128)(2,1)S(1)}, bf16[32,384]{1,0:T(8,128)(2,1)S(1)}, u32[]{:S(2)}, u32[]{:S(2)}) collective-permute-start(bf16[32,384]{1,0:T(8,128)(2,1)S(1)} %get-tuple-element.417), channel_id=1, source_target_pairs={{0,6},{1,7},{2,8},{3,9},{4,10},{5,11},{6,12},{7,13},{8,14},{9,15},... | collective-permute-start | bytes 73736 | tf_op jit(solution)/shard_map/cond/branch_26_fun/ppermute | solution.py:18
  22.1 1.9 %collective-permute-start.52 = (bf16[32,384]{1,0:T(8,128)(2,1)S(1)}, bf16[32,384]{1,0:T(8,128)(2,1)S(1)}, u32[]{:S(2)}, u32[]{:S(2)}) collective-permute-start(bf16[32,384]{1,0:T(8,128)(2,1)S(1)} %get-tuple-element.418), channel_id=1, source_target_pairs={{0,6},{1,7},{2,8},{3,9},{4,10},{5,11},{6,12},{7,13},{8,14},{9,15},... | collective-permute-start | bytes 73736 | tf_op jit(solution)/shard_map/cond/branch_26_fun/ppermute | solution.py:18
  24.0 1.9 %collective-permute-start.53 = (bf16[32,384]{1,0:T(8,128)(2,1)S(1)}, bf16[32,384]{1,0:T(8,128)(2,1)S(1)}, u32[]{:S(2)}, u32[]{:S(2)}) collective-permute-start(bf16[32,384]{1,0:T(8,128)(2,1)S(1)} %get-tuple-element.419), channel_id=1, source_target_pairs={{0,6},{1,7},{2,8},{3,9},{4,10},{5,11},{6,12},{7,13},{8,14},{9,15},... | collective-permute-start | bytes 73736 | tf_op jit(solution)/shard_map/cond/branch_26_fun/ppermute | solution.py:18
  26.0 0.0 collective-permute-done.51
  26.0 3.0 %collective-permute-done.52 = bf16[32,384]{1,0:T(8,128)(2,1)S(1)} collective-permute-done((bf16[32,384]{1,0:T(8,128)(2,1)S(1)}, bf16[32,384]{1,0:T(8,128)(2,1)S(1)}, u32[]{:S(2)}, u32[]{:S(2)}) %collective-permute-start.52) | collective-permute-done | bytes 24608 | tf_op jit(solution)/shard_map/cond/branch_26_fun/ppermute | solution.py:18
  29.0 1.8 %collective-permute-done.53 = bf16[32,384]{1,0:T(8,128)(2,1)S(1)} collective-permute-done((bf16[32,384]{1,0:T(8,128)(2,1)S(1)}, bf16[32,384]{1,0:T(8,128)(2,1)S(1)}, u32[]{:S(2)}, u32[]{:S(2)}) %collective-permute-start.53) | collective-permute-done | bytes 24608 | tf_op jit(solution)/shard_map/cond/branch_26_fun/ppermute | solution.py:18
  30.8 12.1 %conditional.3 = ((bf16[32,384]{1,0:T(8,128)(2,1)S(1)}, bf16[32,384]{1,0:T(8,128)(2,1)S(1)}, bf16[32,384]{1,0:T(8,128)(2,1)S(1)})) conditional(s32[]{:T(128)} %clamp.6, (bf16[32,384]{1,0:T(8,128)(2,1)S(1)}, bf16[32,384]{1,0:T(8,128)(2,1)S(1)}, bf16[32,384]{1,0:T(8,128)(2,1)S(1)}) %get-tuple-element.694, ...), branch_computations={%region_27.28_spmd, %region_28.29_spmd, %region_29.30_spmd, %regio... | conditional | bytes 442520 | solution.py:42
  30.8 7.5 %collective-permute-start.92 = (bf16[32,384]{1,0:T(8,128)(2,1)S(1)}, bf16[32,384]{1,0:T(8,128)(2,1)S(1)}, u32[]{:S(2)}, u32[]{:S(2)}) collective-permute-start(bf16[32,384]{1,0:T(8,128)(2,1)S(1)} %get-tuple-element.480), channel_id=1, source_target_pairs={{0,2},{1,3},{2,4},{3,5},{4,6},{5,7},{6,8},{7,9},{8,10},{9,11},{10,... | collective-permute-start | bytes 73736 | tf_op jit(solution)/shard_map/cond/branch_21_fun/ppermute | solution.py:18
  38.3 1.9 %collective-permute-start.93 = (bf16[32,384]{1,0:T(8,128)(2,1)S(1)}, bf16[32,384]{1,0:T(8,128)(2,1)S(1)}, u32[]{:S(2)}, u32[]{:S(2)}) collective-permute-start(bf16[32,384]{1,0:T(8,128)(2,1)S(1)} %get-tuple-element.481), channel_id=1, source_target_pairs={{0,1},{1,2},{2,3},{3,4},{4,5},{5,6},{6,7},{7,8},{8,9},{9,10},{10,1... | collective-permute-start | bytes 73736 | tf_op jit(solution)/shard_map/cond/branch_21_fun/ppermute | solution.py:18
  40.3 0.0 collective-permute-done.92
  40.3 2.7 %collective-permute-done.93 = bf16[32,384]{1,0:T(8,128)(2,1)S(1)} collective-permute-done((bf16[32,384]{1,0:T(8,128)(2,1)S(1)}, bf16[32,384]{1,0:T(8,128)(2,1)S(1)}, u32[]{:S(2)}, u32[]{:S(2)}) %collective-permute-start.93) | collective-permute-done | bytes 24608 | tf_op jit(solution)/shard_map/cond/branch_21_fun/ppermute | solution.py:18
  43.0 0.0 copy-start.1
  43.0 8.1 %collective-permute-start.108 = (bf16[4,20,384]{2,1,0:T(8,128)(2,1)S(1)}, bf16[4,20,384]{2,1,0:T(8,128)(2,1)S(1)}, u32[]{:S(2)}, u32[]{:S(2)}) collective-permute-start(bf16[4,20,384]{2,1,0:T(8,128)(2,1)S(1)} %get-tuple-element.523), channel_id=1, source_target_pairs={{0,1},{1,2},{2,3},{3,4},{4,5},{5,6},{6,7},{7,8},{8,9},{9,10},{10,1... | collective-permute-start | bytes 184328 | tf_op jit(solution)/shard_map/ppermute | solution.py:50
  51.2 1.9 %collective-permute-start.109 = (bf16[4,20,384]{2,1,0:T(8,128)(2,1)S(1)}, bf16[4,20,384]{2,1,0:T(8,128)(2,1)S(1)}, u32[]{:S(2)}, u32[]{:S(2)}) collective-permute-start(bf16[4,20,384]{2,1,0:T(8,128)(2,1)S(1)} %get-tuple-element.524), channel_id=1, source_target_pairs={{1,0},{2,1},{3,2},{4,3},{5,4},{6,5},{7,6},{8,7},{9,8},{10,9},{11,1... | collective-permute-start | bytes 184328 | tf_op jit(solution)/shard_map/ppermute | solution.py:51
  53.1 0.1 slice.55
  53.2 0.1 rev.3
  53.3 0.1 pad.6.clone
  53.4 0.0 collective-permute-done.108
  53.4 9.7 %collective-permute-done.109 = bf16[4,20,384]{2,1,0:T(8,128)(2,1)S(1)} collective-permute-done((bf16[4,20,384]{2,1,0:T(8,128)(2,1)S(1)}, bf16[4,20,384]{2,1,0:T(8,128)(2,1)S(1)}, u32[]{:S(2)}, u32[]{:S(2)}) %collective-permute-start.109) | collective-permute-done | bytes 61472 | tf_op jit(solution)/shard_map/ppermute | solution.py:51
  63.0 0.1 pad_maximum_fusion.7
  63.2 7.6 %collective-permute-start.110 = (bf16[4,72,20]{2,1,0:T(8,128)(2,1)S(1)}, bf16[4,72,20]{2,1,0:T(8,128)(2,1)S(1)}, u32[]{:S(2)}, u32[]{:S(2)}) collective-permute-start(bf16[4,72,20]{2,1,0:T(8,128)(2,1)S(1)} %get-tuple-element.521), channel_id=1, source_target_pairs={{0,16},{16,32},{32,48},{48,64},{64,80},{80,96},{96,112},{112,128},... | collective-permute-start | bytes 34568 | tf_op jit(solution)/shard_map/ppermute | solution.py:50
  70.8 1.9 %collective-permute-start.111 = (bf16[4,72,20]{2,1,0:T(8,128)(2,1)S(1)}, bf16[4,72,20]{2,1,0:T(8,128)(2,1)S(1)}, u32[]{:S(2)}, u32[]{:S(2)}) collective-permute-start(bf16[4,72,20]{2,1,0:T(8,128)(2,1)S(1)} %get-tuple-element.522), channel_id=1, source_target_pairs={{16,0},{32,16},{48,32},{64,48},{80,64},{96,80},{112,96},{128,112},... | collective-permute-start | bytes 34568 | tf_op jit(solution)/shard_map/ppermute | solution.py:51
  72.7 0.0 copy-start.2
  72.7 0.7 pad_maximum_fusion.8.seed_ref
  73.4 0.6 reshape.13.poly_ref
  74.1 0.0 collective-permute-done.110
  74.1 2.4 %collective-permute-done.111 = bf16[4,72,20]{2,1,0:T(8,128)(2,1)S(1)} collective-permute-done((bf16[4,72,20]{2,1,0:T(8,128)(2,1)S(1)}, bf16[4,72,20]{2,1,0:T(8,128)(2,1)S(1)}, u32[]{:S(2)}, u32[]{:S(2)}) %collective-permute-start.111) | collective-permute-done | bytes 11552 | tf_op jit(solution)/shard_map/ppermute | solution.py:51
  76.5 0.2 pad_maximum_fusion
  76.7 0.8 pad.4.window_ref
  77.5 8.5 %coadd.1 = (f32[32,384]{1,0:T(8,128)}, f32[32,384]{1,0:T(8,128)}) custom-call(f32[120]{0:T(128)} %reshape.13.poly_ref, f32[4]{0:T(128)} %weight_ref.1, s32[4]{0:T(128)} %start_ref.1, s32[4]{0:T(128)} %count_ref.1, f32[21]{0:T(128)} %taps_ref.1, bf16[4,80,512]{2,1,0:T(8,128)(2,1)} %pad.4.window_ref, f32[105,128]{1,0:T(8,128)} %pad_maximum_fusion.8.seed_ref), custom_call_target="tpu_custom_call" | custom-call | tf_op jit(solution)/shard_map/coadd/pallas_call | solution.py:217
  (15 shorter events, 0.1 us)
Async XLA Ops:
  0.6 9.1 %copy-start = (bf16[4,32,384]{2,1,0:T(8,128)(2,1)S(1)}, bf16[4,32,384]{2,1,0:T(8,128)(2,1)}, u32[]{:S(2)}) copy-start(bf16[4,32,384]{2,1,0:T(8,128)(2,1)} %param.61) | copy-start | bytes 294916
  9.9 16.1 %collective-permute-start.51 = (bf16[32,384]{1,0:T(8,128)(2,1)S(1)}, bf16[32,384]{1,0:T(8,128)(2,1)S(1)}, u32[]{:S(2)}, u32[]{:S(2)}) collective-permute-start(bf16[32,384]{1,0:T(8,128)(2,1)S(1)} %get-tuple-element.417), channel_id=1, source_target_pairs={{0,6},{1,7},{2,8},{3,9},{4,10},{5,11},{6,12},{7,13},{8,14},{9,15},... | collective-permute-start | bytes 73736 | tf_op jit(solution)/shard_map/cond/branch_26_fun/ppermute | solution.py:18
  22.1 6.9 %collective-permute-start.52 = (bf16[32,384]{1,0:T(8,128)(2,1)S(1)}, bf16[32,384]{1,0:T(8,128)(2,1)S(1)}, u32[]{:S(2)}, u32[]{:S(2)}) collective-permute-start(bf16[32,384]{1,0:T(8,128)(2,1)S(1)} %get-tuple-element.418), channel_id=1, source_target_pairs={{0,6},{1,7},{2,8},{3,9},{4,10},{5,11},{6,12},{7,13},{8,14},{9,15},... | collective-permute-start | bytes 73736 | tf_op jit(solution)/shard_map/cond/branch_26_fun/ppermute | solution.py:18
  24.0 6.8 %collective-permute-start.53 = (bf16[32,384]{1,0:T(8,128)(2,1)S(1)}, bf16[32,384]{1,0:T(8,128)(2,1)S(1)}, u32[]{:S(2)}, u32[]{:S(2)}) collective-permute-start(bf16[32,384]{1,0:T(8,128)(2,1)S(1)} %get-tuple-element.419), channel_id=1, source_target_pairs={{0,6},{1,7},{2,8},{3,9},{4,10},{5,11},{6,12},{7,13},{8,14},{9,15},... | collective-permute-start | bytes 73736 | tf_op jit(solution)/shard_map/cond/branch_26_fun/ppermute | solution.py:18
  30.8 9.4 %collective-permute-start.92 = (bf16[32,384]{1,0:T(8,128)(2,1)S(1)}, bf16[32,384]{1,0:T(8,128)(2,1)S(1)}, u32[]{:S(2)}, u32[]{:S(2)}) collective-permute-start(bf16[32,384]{1,0:T(8,128)(2,1)S(1)} %get-tuple-element.480), channel_id=1, source_target_pairs={{0,2},{1,3},{2,4},{3,5},{4,6},{5,7},{6,8},{7,9},{8,10},{9,11},{10,... | collective-permute-start | bytes 73736 | tf_op jit(solution)/shard_map/cond/branch_21_fun/ppermute | solution.py:18
  38.3 4.6 %collective-permute-start.93 = (bf16[32,384]{1,0:T(8,128)(2,1)S(1)}, bf16[32,384]{1,0:T(8,128)(2,1)S(1)}, u32[]{:S(2)}, u32[]{:S(2)}) collective-permute-start(bf16[32,384]{1,0:T(8,128)(2,1)S(1)} %get-tuple-element.481), channel_id=1, source_target_pairs={{0,1},{1,2},{2,3},{3,4},{4,5},{5,6},{6,7},{7,8},{8,9},{9,10},{10,1... | collective-permute-start | bytes 73736 | tf_op jit(solution)/shard_map/cond/branch_21_fun/ppermute | solution.py:18
  43.0 10.1 %copy-start.1 = (bf16[5,21,21]{2,1,0:T(8,128)(2,1)S(1)}, bf16[5,21,21]{2,1,0:T(8,128)(2,1)}, u32[]{:S(2)}) copy-start(bf16[5,21,21]{2,1,0:T(8,128)(2,1)} %param.62) | copy-start | bytes 13234
  43.0 10.3 %collective-permute-start.108 = (bf16[4,20,384]{2,1,0:T(8,128)(2,1)S(1)}, bf16[4,20,384]{2,1,0:T(8,128)(2,1)S(1)}, u32[]{:S(2)}, u32[]{:S(2)}) collective-permute-start(bf16[4,20,384]{2,1,0:T(8,128)(2,1)S(1)} %get-tuple-element.523), channel_id=1, source_target_pairs={{0,1},{1,2},{2,3},{3,4},{4,5},{5,6},{6,7},{7,8},{8,9},{9,10},{10,1... | collective-permute-start | bytes 184328 | tf_op jit(solution)/shard_map/ppermute | solution.py:50
  51.2 11.9 %collective-permute-start.109 = (bf16[4,20,384]{2,1,0:T(8,128)(2,1)S(1)}, bf16[4,20,384]{2,1,0:T(8,128)(2,1)S(1)}, u32[]{:S(2)}, u32[]{:S(2)}) collective-permute-start(bf16[4,20,384]{2,1,0:T(8,128)(2,1)S(1)} %get-tuple-element.524), channel_id=1, source_target_pairs={{1,0},{2,1},{3,2},{4,3},{5,4},{6,5},{7,6},{8,7},{9,8},{10,9},{11,1... | collective-permute-start | bytes 184328 | tf_op jit(solution)/shard_map/ppermute | solution.py:51
  63.2 10.9 %collective-permute-start.110 = (bf16[4,72,20]{2,1,0:T(8,128)(2,1)S(1)}, bf16[4,72,20]{2,1,0:T(8,128)(2,1)S(1)}, u32[]{:S(2)}, u32[]{:S(2)}) collective-permute-start(bf16[4,72,20]{2,1,0:T(8,128)(2,1)S(1)} %get-tuple-element.521), channel_id=1, source_target_pairs={{0,16},{16,32},{32,48},{48,64},{64,80},{80,96},{96,112},{112,128},... | collective-permute-start | bytes 34568 | tf_op jit(solution)/shard_map/ppermute | solution.py:50
  70.8 5.7 %collective-permute-start.111 = (bf16[4,72,20]{2,1,0:T(8,128)(2,1)S(1)}, bf16[4,72,20]{2,1,0:T(8,128)(2,1)S(1)}, u32[]{:S(2)}, u32[]{:S(2)}) collective-permute-start(bf16[4,72,20]{2,1,0:T(8,128)(2,1)S(1)} %get-tuple-element.522), channel_id=1, source_target_pairs={{16,0},{32,16},{48,32},{64,48},{80,64},{96,80},{112,96},{128,112},... | collective-permute-start | bytes 34568 | tf_op jit(solution)/shard_map/ppermute | solution.py:51
  72.7 0.7 copy-start.2

commit v2 on v1

--- a/solution.py
+++ b/solution.py
@@ -11,45 +11,249 @@
 SUBLANES = 8
 
 
-def moved(array, shift):
-    peers = lax.axis_size("narrow")
-    if shift == 0:
-        return array
-    return lax.ppermute(array, "narrow", [(i, i + shift) for i in range(peers - shift)])
-
-
-def placed_tiles(tiles, shifts, radix):
-    for scale, digits in (
-        (radix, [shift // radix for shift in shifts]),
-        (1, [shift % radix for shift in shifts]),
-    ):
-        choice = digits[0]
-        for digit in digits[1:]:
-            choice = choice * radix + digit
-
-        def branch(index, scale=scale):
-            own = []
-            for _ in tiles:
-                own.append(index % radix)
-                index //= radix
-            own = own[::-1]
-
-            def run(*operands):
-                return tuple(moved(op, scale * step) for op, step in zip(operands, own))
-
-            return run
-
-        tiles = lax.switch(choice, [branch(i) for i in range(radix ** len(tiles))], *tiles)
-    return tiles
-
-
-def padded(array, axis, dim, width):
-    peers, length = lax.axis_size(axis), array.shape[dim]
-    up = [(i, i + 1) for i in range(peers - 1)]
-    down = [(j, i) for i, j in up]
-    before = lax.ppermute(lax.slice_in_dim(array, length - width, length, axis=dim), axis, up)
-    after = lax.ppermute(lax.slice_in_dim(array, 0, width, axis=dim), axis, down)
-    return jnp.concatenate([before, array, after], axis=dim)
+MESH = pl.DeviceIdType.MESH
+
+
+def exchange_kernel(
+    shift_ref, x_ref, window, left, right, far, near, across, cross, held, sent, got, column_sem
+):
+    members, tile_rows = x_ref.shape[:2]
+    ring = lax.axis_size("narrow") // 2
+    me = lax.axis_index("narrow")
+    column, columns = lax.axis_index("wide"), lax.axis_size("wide")
+    second, place = me // ring, me % ring
+
+    def on_ring(turn):
+        return {"narrow": second * ring + (place + turn + ring) % ring}
+
+    last_first = (second == 0) & (place == ring - 1)
+    first_second = (second == 1) & (place == 0)
+    last_second = (second == 1) & (place == ring - 1)
+    other = {"narrow": (1 - second) * ring + place}
+    over_end = {"narrow": (1 - second) * ring + (ring - 1 - place)}
+
+    barrier = pltpu.get_barrier_semaphore()
+    for peer in (on_ring(1), on_ring(-1), on_ring(3), on_ring(-3), other):
+        pl.semaphore_signal(barrier, inc=1, device_id=peer, device_id_type=MESH)
+
+    @pl.when(last_first | first_second)
+    def _():
+        pl.semaphore_signal(barrier, inc=1, device_id=over_end, device_id_type=MESH)
+
+    @pl.when(column > 0)
+    def _():
+        pl.semaphore_signal(barrier, inc=1, device_id={"wide": column - 1}, device_id_type=MESH)
+
+    @pl.when(column < columns - 1)
+    def _():
+        pl.semaphore_signal(barrier, inc=1, device_id={"wide": column + 1}, device_id_type=MESH)
+
+    count = 5 + (last_first | first_second).astype(jnp.int32)
+    count = count + (column > 0).astype(jnp.int32) + (column < columns - 1).astype(jnp.int32)
+    pl.semaphore_wait(barrier, count)
+
+    def copy(src, dst, slot, peer):
+        return pltpu.make_async_remote_copy(
+            src_ref=src,
+            dst_ref=dst,
+            send_sem=sent.at[slot],
+            recv_sem=got.at[slot],
+            device_id=peer,
+            device_id_type=MESH,
+        )
+
+    def own(e):
+        return window.at[e, tile_rows : 2 * tile_rows, :]
+
+    def turns(src, into, slot, e, by):
+        return [
+            copy(src, into.at[e, i], slot + 2 * e + i, on_ring(turn))
+            for i, turn in enumerate((by, -by))
+        ]
+
+    def pick(e, digit, stay, moved):
+        value = jnp.full(stay.shape, shift_ref[2 * e + digit], jnp.int32)
+        up, down = moved[e, 0].astype(jnp.float32), moved[e, 1].astype(jnp.float32)
+        chosen = jnp.where(value == 1, up, jnp.where(value == -1, down, stay.astype(jnp.float32)))
+        return chosen.astype(jnp.bfloat16)
+
+    window[0, tile_rows : 2 * tile_rows, :] = x_ref[0]
+
+    def rows_out(e):
+        above = copy(own(e), window.at[e, 0:tile_rows, :], 16 + 2 * e, on_ring(1))
+        below = copy(
+            own(e), window.at[e, 2 * tile_rows : 3 * tile_rows, :], 17 + 2 * e, on_ring(-1)
+        )
+        return above, below
+
+    def wrapped(e):
+        return copy(across.at[e], window.at[e, 0:tile_rows, :], 16 + 2 * e, on_ring(1))
+
+    def over(e):
+        return copy(window.at[e, tile_rows : 2 * tile_rows, :], across.at[e], 24 + e, other)
+
+    def end(e):
+        return copy(x_ref.at[e], cross.at[e], 28 + e, over_end)
+
+    first = [turns(x_ref.at[e], far, 0, e, 3) for e in range(1, members)]
+    for pair in first:
+        for c in pair:
+            c.start()
+
+    @pl.when(first_second)
+    def _():
+        for e in range(members):
+            end(e).start()
+
+    @pl.when(last_first)
+    def _():
+        over(0).start()
+
+    second_turns = []
+    for e in range(1, members):
+        for c in first[e - 1]:
+            c.wait_recv()
+        held[e] = pick(e, 0, x_ref[e], far)
+        pair = turns(held.at[e], near, 8, e, 1)
+        for c in pair:
+            c.start()
+        second_turns.append(pair)
+    for e in range(1, members):
+        for c in second_turns[e - 1]:
+            c.wait_recv()
+        window[e, tile_rows : 2 * tile_rows, :] = pick(e, 1, held[e], near)
+
+        @pl.when(second == 0)
+        def _(e=e):
+            over(e).start()
+
+    @pl.when(last_second)
+    def _():
+        over(0).wait_recv()
+        wrapped(0).start()
+
+    @pl.when(jnp.logical_not(last_second))
+    def _():
+        rows_out(0)[0].start()
+
+    rows_out(0)[1].start()
+    for e in range(1, members):
+
+        @pl.when(second == 1)
+        def _(e=e):
+            over(e).wait_recv()
+            here = window[e, tile_rows : 2 * tile_rows, :].astype(jnp.float32)
+            passed = jnp.full(here.shape, shift_ref[2 * members + e] - place, jnp.int32)
+            chosen = jnp.where(passed > 0, across[e].astype(jnp.float32), here)
+            window[e, tile_rows : 2 * tile_rows, :] = chosen.astype(jnp.bfloat16)
+
+        @pl.when(last_second)
+        def _(e=e):
+            wrapped(e).start()
+
+        @pl.when(jnp.logical_not(last_second))
+        def _(e=e):
+            rows_out(e)[0].start()
+
+        rows_out(e)[1].start()
+
+    for e in range(members):
+        for c in rows_out(e):
+            c.wait_recv()
+
+    @pl.when(last_first)
+    def _():
+        for e in range(members):
+            end(e).wait_recv()
+            here = window[e, 2 * tile_rows : 3 * tile_rows, :].astype(jnp.float32)
+            still = jnp.full(here.shape, shift_ref[2 * members + e], jnp.int32)
+            chosen = jnp.where(still == 0, cross[e].astype(jnp.float32), here)
+            window[e, 2 * tile_rows : 3 * tile_rows, :] = chosen.astype(jnp.bfloat16)
+
+    width = window.shape[2]
+
+    def sideways(lanes, into, slot, peer):
+        return pltpu.make_async_remote_copy(
+            src_ref=window.at[:, :, lanes : lanes + LANES],
+            dst_ref=into,
+            send_sem=column_sem.at[slot],
+            recv_sem=column_sem.at[2 + slot],
+            device_id={"wide": peer},
+            device_id_type=MESH,
+        )
+
+    to_left = sideways(0, right, 0, column - 1)
+    to_right = sideways(width - LANES, left, 1, column + 1)
+
+    @pl.when(column > 0)
+    def _():
+        to_left.start()
+
+    @pl.when(column < columns - 1)
+    def _():
+        to_right.start()
+
+    for e in range(1, members):
+        for c in first[e - 1] + second_turns[e - 1]:
+            c.wait_send()
+    for e in range(members):
+        for c in rows_out(e):
+            c.wait_send()
+
+    @pl.when(second == 0)
+    def _():
+        for e in range(1, members):
+            over(e).wait_send()
+
+    @pl.when(last_first)
+    def _():
+        over(0).wait_send()
+
+    @pl.when(first_second)
+    def _():
+        for e in range(members):
+            end(e).wait_send()
+
+    @pl.when(column > 0)
+    def _():
+        to_left.wait_send()
+        to_right.wait_recv()
+
+    @pl.when(column < columns - 1)
+    def _():
+        to_right.wait_send()
+        to_left.wait_recv()
+
+
+def exchange(exposures, row_start):
+    members, tile_rows, tile_cols = exposures.shape
+    ring = lax.axis_size("narrow") // 2
+    moves = row_start // tile_rows
+    turn = (moves + ring // 2 - 1) % ring - (ring // 2 - 1)
+    high = (turn >= 2).astype(jnp.int32) - (turn <= -2).astype(jnp.int32)
+    digits = jnp.stack([high, turn - 3 * high], axis=1).reshape(-1)
+    dtype = exposures.dtype
+    vmem = pl.BlockSpec(memory_space=pltpu.VMEM)
+    edge = jax.ShapeDtypeStruct((members, 3 * tile_rows, LANES), dtype)
+    tile = (members, tile_rows, tile_cols)
+    return pl.pallas_call(
+        exchange_kernel,
+        out_shape=(jax.ShapeDtypeStruct((members, 3 * tile_rows, tile_cols), dtype), edge, edge),
+        in_specs=[pl.BlockSpec(memory_space=pltpu.SMEM), vmem],
+        out_specs=(vmem,) * 3,
+        scratch_shapes=[
+            pltpu.VMEM((members, 2, tile_rows, tile_cols), dtype),
+            pltpu.VMEM((members, 2, tile_rows, tile_cols), dtype),
+            pltpu.VMEM(tile, dtype),
+            pltpu.VMEM(tile, dtype),
+            pltpu.VMEM(tile, dtype),
+            pltpu.SemaphoreType.DMA((32,)),
+            pltpu.SemaphoreType.DMA((32,)),
+            pltpu.SemaphoreType.DMA((4,)),
+        ],
+        compiler_params=pltpu.CompilerParams(collective_id=0, has_side_effects=True),
+        name="exchange",
+    )(jnp.concatenate([digits, moves]), exposures)
 
 
 def coadd_kernel(
@@ -60,6 +264,8 @@
     count_ref,
     taps_ref,
     window_ref,
+    left_ref,
+    right_ref,
     seed_ref,
     coadd_ref,
     detect_ref,
@@ -85,9 +291,9 @@
                 jnp.bfloat16
             )
 
-    all_rows = shifted.shape[1]
+    all_rows, lead = shifted.shape[1], tile_rows - 2 * half
     window_rows = (
-        row_base - 2 * half + lax.broadcasted_iota(jnp.int32, (all_rows, LANES), 0)
+        row_base - tile_rows + lax.broadcasted_iota(jnp.int32, (all_rows, LANES), 0)
     )
     lane_in = lax.broadcasted_iota(jnp.int32, (all_rows, LANES), 1)
     out_row = row_base - half + lax.broadcasted_iota(jnp.int32, (rows, LANES), 0)
@@ -108,11 +314,16 @@
         def _(e=e, first=first, total=total, weighting=weighting):
             valid = (window_rows >= first) & (window_rows < first + total)
             parts = []
+            pieces = [left_ref[e]]
             for tile in range(window_ref.shape[2] // LANES):
-                part = window_ref[e, :, tile * LANES : (tile + 1) * LANES].astype(jnp.float32)
-                parts.append(jnp.where(valid, part, 0.0))
+                pieces.append(window_ref[e, :, tile * LANES : (tile + 1) * LANES])
+            pieces.append(right_ref[e])
+            for tile, piece in enumerate(pieces):
+                col = lane_in + (col_base + (tile - 1) * LANES)
+                keep = valid & (col >= 0) & (col < band_cols)
+                parts.append(jnp.where(keep, piece.astype(jnp.float32), 0.0))
             for block in range(blocks):
-                tile, offset = divmod(block * step, LANES)
+                tile, offset = divmod(LANES - 2 * half + block * step, LANES)
                 here = parts[tile]
                 if offset:
                     here = pltpu.roll(here, LANES - offset, 1)
@@ -124,7 +335,8 @@
                 shifted[block] = here
             for a in range(side):
                 piece = jnp.concatenate(
-                    [shifted[block, a : a + rows, :] for block in range(blocks)], axis=0
+                    [shifted[block, lead + a : lead + a + rows, :] for block in range(blocks)],
+                    axis=0,
                 )
                 lhs[:, a * LANES : (a + 1) * LANES] = piece.astype(jnp.bfloat16)
             response = jnp.dot(lhs[...], table[...], preferred_element_type=jnp.float32)
@@ -196,17 +408,10 @@
     step = LANES - (side - 1)
     blocks = pl.cdiv(tile_cols + 2 * half, step)
     rows = pl.cdiv(tile_rows + 2 * half, SUBLANES) * SUBLANES
-    all_rows = pl.cdiv(rows + side - 1, 2 * SUBLANES) * 2 * SUBLANES
-
-    shifts = [row_start[e] // tile_rows for e in range(1, members)]
-    tiles = placed_tiles(tuple(exposures[e] for e in range(1, members)), shifts, 3)
-    window = jnp.stack([exposures[0], *tiles])
-    window = padded(window, "narrow", 1, 2 * half)
-    window = padded(window, "wide", 2, 2 * half)
-    width = pl.cdiv(tile_cols + 4 * half, LANES) * LANES
-    window = jnp.pad(
-        window, ((0, 0), (0, all_rows - window.shape[1]), (0, width - window.shape[2]))
-    )
+    all_rows = 3 * tile_rows
+
+    window, left, right = exchange(exposures, row_start)
+    width = pl.cdiv(tile_cols + 2 * half, LANES) * LANES
     taps = basis_kernels.astype(jnp.float32).reshape(kernels * side, side)
     seed = jnp.concatenate(
         [taps[:, :1], jnp.zeros((kernels * side, step - 1), jnp.float32), taps[:, :0:-1]], axis=1
@@ -217,7 +422,7 @@
     return pl.pallas_call(
         functools.partial(coadd_kernel, sizes),
         out_shape=(out, out),
-        in_specs=[scalars] * 5 + [pl.BlockSpec(memory_space=pltpu.VMEM)] * 2,
+        in_specs=[scalars] * 5 + [pl.BlockSpec(memory_space=pltpu.VMEM)] * 4,
         out_specs=(pl.BlockSpec(memory_space=pltpu.VMEM),) * 2,
         scratch_shapes=[
             pltpu.VMEM((side * LANES, kernels * LANES), jnp.bfloat16),
@@ -234,6 +439,8 @@
         row_count,
         filter_taps,
         window,
+        left,
+        right,
         seed,
     )
 

time: 87.7 us -> 44.5 us (0.51); the launches traced: 86 us -> 44.3 us
  starting transfers between devices: 45 us -> 0 us
  Pallas kernels: 8.5 us -> 40.7 us
  waiting for transfers between devices: 19.6 us -> 0 us
  between operations: 8.53 us -> 0.69 us
  local copies, waits for them, and re-layouts: 3.1 us -> 1.58 us
    ppermute x9 -> x0, starting transfers between devices: 45 us -> none  [the longest x5 25.5 us: moved(): lax.ppermute(array, 'narrow', [(i, i + shift) for i in range(peers - shif...]
    pallas_call x0 -> x1, Pallas kernels: none -> 32.3 us  [exchange(): pl.pallas_call(exchange_kernel, out_shape=(jax.ShapeDtypeStruct((members,...]
    ppermute x9 -> x0, waiting for transfers between devices: 19.6 us -> none  [the longest x2 12.1 us: padded(): lax.ppermute(lax.slice_in_dim(array, 0, width, axis=dim), axis, down)]
    slice x3 -> x0, local copies, waits for them, and re-layouts: 1.4 us -> none  [the longest x1 1.36 us: on_device(): shifts = [row_start[e] // tile_rows for e in range(1, members)]]
  transfers between devices with their start and end apart: 9 -> 0, of which waited for: 5 -> 0; matrix products, arithmetic and copies ran while one was open for 2% -> 0% of each run, Pallas kernels for 0% -> 0%
where the time goes in v2:
time: 44.5 us; the launch traced here: 44.3 us
  Pallas kernels  40.7 us (91%)
  local copies, waits for them, and re-layouts  1.58 us (4%)
  other arithmetic  1.34 us (3%)
  between operations  0.69 us (2%)
    pallas_call x1, Pallas kernels, exchange(): pl.pallas_call(exchange_kernel, out_shape=(jax.ShapeDtypeStruct((members,...  32.3 us
    pallas_call x1, Pallas kernels, on_device(): pl.pallas_call(functools.partial(coadd_kernel, sizes), out_shape=(out, ou...  8.4 us

profile of v2, /device:TPU:57, one launch (start us, length us, event | category | flops | bytes accessed | tf_op | source)
XLA Modules:
  0.0 44.3 jit_solution(10908443503415114001)
XLA Ops:
  0.6 0.0 copy-start.2
  0.7 0.0 copy-start.1
  0.7 0.1 pad.1.clone
  0.7 0.5 %copy-done.2 = s32[4]{0:T(128)S(1)} copy-done((s32[4]{0:T(128)S(1)}, s32[4]{0:T(128)}, u32[]{:S(2)}) %copy-start.2) | copy-done | bytes 40
  1.3 0.0 copy-start
  1.3 0.1 copy.12
  1.4 0.1 reshape.17
  1.5 0.6 %pad_add_fusion.1.shift_ref = s32[12]{0:T(128)} fusion(s32[4]{0:T(128)S(1)} %get-tuple-element.10, s32[8]{0:T(128)S(1)} %reshape.17), kind=kLoop, calls=%fused_computation.14 | loop fusion | flops 12 | bytes 96 | tf_op jit(solution)/shard_map/concatenate | solution.py:256
  2.1 0.0 copy-done.1
  2.1 0.6 %reshape.16.poly_ref = f32[120]{0:T(128)} reshape(f32[4,5,6]{2,1,0:T(8,128)S(1)} %copy.11) | data formatting | bytes 960 | tf_op jit(solution)/shard_map/reshape | solution.py:436
  2.7 0.0 copy-done
  2.7 0.1 slice.9
  2.8 0.1 rev.3
  2.9 0.7 %pad_maximum_fusion.seed_ref = f32[105,128]{1,0:T(8,128)} fusion(f32[105,20]{1,0:T(8,128)S(1)} %rev.3, f32[105,1]{1,0:T(8,128)S(1)} %bitcast.5, f32[128]{0:T(128)S(1)} %pad.1.clone), kind=kLoop, calls=%fused_computation | loop fusion | flops 26880 | bytes 63092 | tf_op jit(solution)/shard_map/concatenate | solution.py:416
  3.6 32.3 %exchange.1 = (bf16[4,96,384]{2,1,0:T(8,128)(2,1)}, bf16[4,96,128]{2,1,0:T(8,128)(2,1)}, bf16[4,96,128]{2,1,0:T(8,128)(2,1)}) custom-call(s32[12]{0:T(128)} %pad_add_fusion.1.shift_ref, bf16[4,32,384]{2,1,0:T(8,128)(2,1)} %x_ref.1), custom_call_target="tpu_custom_call" | custom-call | tf_op jit(solution)/shard_map/exchange/pallas_call | solution.py:239
  35.9 8.4 %coadd.1 = (f32[32,384]{1,0:T(8,128)}, f32[32,384]{1,0:T(8,128)}) custom-call(f32[120]{0:T(128)} %reshape.16.poly_ref, f32[4]{0:T(128)} %weight_ref.1, s32[4]{0:T(128)} %start_ref.1, s32[4]{0:T(128)} %count_ref.1, f32[21]{0:T(128)} %taps_ref.1, bf16[4,96,384]{2,1,0:T(8,128)(2,1)} %get-tuple-element.5.window_ref, ...), custom_call_target="tpu_custom_call" | custom-call | tf_op jit(solution)/shard_map/coadd/pallas_call | solution.py:422
  (6 shorter events, 0.1 us)
Async XLA Ops:
  0.6 0.7 %copy-start.2 = (s32[4]{0:T(128)S(1)}, s32[4]{0:T(128)}, u32[]{:S(2)}) copy-start(s32[4]{0:T(128)} %start_ref.1) | copy-start | bytes 52
  0.7 1.5 %copy-start.1 = (f32[4,5,6]{2,0,1:T(4,128)S(1)}, f32[4,5,6]{2,0,1:T(4,128)}, u32[]{:S(2)}) copy-start(f32[4,5,6]{2,0,1:T(4,128)} %param.9) | copy-start | bytes 1444
  1.3 1.4 %copy-start = (bf16[5,21,21]{2,1,0:T(8,128)(2,1)S(1)}, bf16[5,21,21]{2,1,0:T(8,128)(2,1)}, u32[]{:S(2)}) copy-start(bf16[5,21,21]{2,1,0:T(8,128)(2,1)} %param.8) | copy-start | bytes 13234

commit v3 on v1

v3 whole, which is shorter than its diff:
```python
import functools

import jax
import jax.numpy as jnp
from jax import lax
from jax.experimental import pallas as pl
from jax.experimental.pallas import tpu as pltpu
from jax.sharding import PartitionSpec as P

LANES = 128
SUBLANES = 8


MESH = pl.DeviceIdType.MESH
BF16 = jnp.bfloat16


def whole_kernel(
    sizes,
    poly_ref,
    weight_ref,
    start_ref,
    count_ref,
    taps_ref,
    x_ref,
    basis_ref,
    coadd_ref,
    detect_ref,
    window,
    edges,
    far,
    near,
    across,
    cross,
    cross_edges,
    held,
    table,
    shifted,
    lhs,
    sums,
    spread,
    turn_sent,
    turn_got,
    over_sent,
    over_got,
    end_sent,
    end_got,
    ship_sent,
    ship_got,
):
    members, kernels, side, band_rows, band_cols, tile_rows, tile_cols = sizes
    half = side // 2
    step = LANES - (side - 1)
    blocks = pl.cdiv(tile_cols + 2 * half, step)
    rows = pl.cdiv(tile_rows + 2 * half, SUBLANES) * SUBLANES
    ring = lax.axis_size("narrow") // 2
    me = lax.axis_index("narrow")
    column, columns = lax.axis_index("wide"), lax.axis_size("wide")
    second, place = me // ring, me % ring
    row_base, col_base = me * tile_rows, column * tile_cols
    has = (column > 0, column < columns - 1)

    def on_ring(turn):
        return second * ring + (place + turn + ring) % ring

    last_first = (second == 0) & (place == ring - 1)
    first_second = (second == 1) & (place == 0)
    last_second = (second == 1) & (place == ring - 1)
    other = (1 - second) * ring + place
    over_end = (1 - second) * ring + (ring - 1 - place)

    barrier = pltpu.get_barrier_semaphore()

    def greet(peer):
        pl.semaphore_signal(barrier, inc=1, device_id=peer, device_id_type=MESH)

    for peer in (on_ring(3), on_ring(-3), other):
        greet({"narrow": peer})
    for turn in (1, -1):
        greet({"narrow": on_ring(turn)})
    at_end = last_first | first_second
    count = 5 + at_end.astype(jnp.int32)

    @pl.when(at_end)
    def _():
        greet({"narrow": over_end})

    for i in range(2):
        beside = column + 2 * i - 1

        @pl.when(has[i])
        def _(beside=beside):
            greet({"wide": beside})
            for turn in (1, -1):
                greet({"narrow": on_ring(turn), "wide": beside})

        @pl.when(has[i] & at_end)
        def _(beside=beside):
            greet({"narrow": over_end, "wide": beside})

        count = count + 3 * has[i].astype(jnp.int32) + (has[i] & at_end).astype(jnp.int32)

    tap = lax.broadcasted_iota(jnp.int32, (side, LANES), 0)
    spot = lax.broadcasted_iota(jnp.int32, (side, LANES), 1)
    reverse = jnp.where((tap + spot == LANES) | (tap + spot == 0), 1.0, 0.0).astype(BF16)
    for k in range(kernels):
        seeds = jnp.dot(basis_ref[k], reverse, preferred_element_type=jnp.float32)
        for a in range(side):
            seed = jnp.broadcast_to(seeds[a : a + 1, :], (LANES, LANES))
            band = pltpu.roll(seed, 0, 1, stride=1, stride_axis=0)
            table[a * LANES : (a + 1) * LANES, k * LANES : (k + 1) * LANES] = band.astype(BF16)
    window[0, tile_rows : 2 * tile_rows, :] = x_ref[0]

    pl.semaphore_wait(barrier, count)

    def copy(src, dst, send_sem, recv_sem, peer):
        return pltpu.make_async_remote_copy(
            src_ref=src,
            dst_ref=dst,
            send_sem=send_sem,
            recv_sem=recv_sem,
            device_id=peer,
            device_id_type=MESH,
        )

    def own(e):
        return window.at[e, tile_rows : 2 * tile_rows, :]

    def turned(e, stage, i):
        src, into, by = ((x_ref, far, 3), (held, near, 1))[stage]
        slot = (2 * e + stage) * 2 + i
        peer = {"narrow": on_ring(by - 2 * by * i)}
        return copy(src.at[e], into.at[e, i], turn_sent.at[slot], turn_got.at[slot], peer)

    def over(e):
        return copy(own(e), across.at[e], over_sent.at[e], over_got.at[e], {"narrow": other})

    def lanes_of(i):
        return slice(0, LANES) if i == 0 else slice(tile_cols - LANES, tile_cols)

    def end(i):
        if i == 2:
            return copy(x_ref, cross, end_sent.at[2], end_got.at[2], {"narrow": over_end})
        return copy(
            x_ref.at[:, :, lanes_of(i)],
            cross_edges.at[1 - i],
            end_sent.at[i],
            end_got.at[i],
            {"narrow": over_end, "wide": column + 2 * i - 1},
        )

    def parcel(e, n, i, src):
        slot = (3 * e + n) * 3 + i
        where = slice(n * tile_rows, (n + 1) * tile_rows)
        peer = {"narrow": on_ring(1 - n)} if n != 1 else {}
        if i == 2:
            dst = window.at[e, where, :]
        else:
            peer["wide"] = column + 2 * i - 1
            src, dst = src.at[:, lanes_of(i)], edges.at[1 - i, e, where, :]
        return copy(src, dst, ship_sent.at[slot], ship_got.at[slot], peer)

    def each(e, src, steps, act):
        for n in steps:
            for i in (2, 0, 1):
                if i == 2:
                    if n != 1:
                        act(n, i, src)
                else:

                    @pl.when(has[i])
                    def _(n=n, i=i):
                        act(n, i, src)

    def ship(e, steps):
        if 0 in steps:

            @pl.when(last_second)
            def _():
                each(e, across.at[e], (0,), lambda n, i, src: parcel(e, n, i, src).start())

            @pl.when(jnp.logical_not(last_second))
            def _():
                each(e, own(e), (0,), lambda n, i, src: parcel(e, n, i, src).start())

        rest = tuple(n for n in steps if n)
        each(e, own(e), rest, lambda n, i, src: parcel(e, n, i, src).start())

    def arrive(e):
        for n in (0, 2):
            parcel(e, n, 2, own(e)).wait_recv()
        for i in range(2):

            @pl.when(has[1 - i])
            def _(i=i):
                for n in range(3):
                    parcel(e, n, i, own(e)).wait_recv()

    def choose(value, wanted, yes, no):
        test = jnp.full(no.shape, value, jnp.int32)
        return jnp.where(test == wanted, yes.astype(jnp.float32), no.astype(jnp.float32)).astype(BF16)

    moves = [start_ref[e] // tile_rows for e in range(members)]
    turns = [jnp.where(m > ring // 2, m - ring, m) for m in moves]
    high = [jnp.where(t >= 2, 1, jnp.where(t <= -2, -1, 0)) for t in turns]
    low = [t - 3 * h for t, h in zip(turns, high)]

    for e in range(1, members):
        for i in range(2):
            turned(e, 0, i).start()

    @pl.when(last_first)
    def _():
        over(0).start()

    ship(0, (1, 2))

    @pl.when(jnp.logical_not(last_second))
    def _():
        each(0, own(0), (0,), lambda n, i, src: parcel(0, n, i, src).start())

    @pl.when(first_second)
    def _():
        end(2).start()

    for i in range(2):

        @pl.when(first_second & has[i])
        def _(i=i):
            end(i).start()

    for e in range(1, members):
        for i in range(2):
            turned(e, 0, i).wait_recv()
        held[e] = choose(high[e], 1, far[e, 0], choose(high[e], -1, far[e, 1], x_ref[e]))
        for i in range(2):
            turned(e, 1, i).start()

    @pl.when(last_second)
    def _():
        over(0).wait_recv()
        each(0, across.at[0], (0,), lambda n, i, src: parcel(0, n, i, src).start())

    for e in range(1, members):
        for i in range(2):
            turned(e, 1, i).wait_recv()
        window[e, tile_rows : 2 * tile_rows, :] = choose(
            low[e], 1, near[e, 0], choose(low[e], -1, near[e, 1], held[e])
        )

        @pl.when(second == 0)
        def _(e=e):
            over(e).start()
            ship(e, (0, 1, 2))

    all_rows, lead = shifted.shape[1], tile_rows - 2 * half
    window_rows = row_base - tile_rows + lax.broadcasted_iota(jnp.int32, (all_rows, LANES), 0)
    lane_in = lax.broadcasted_iota(jnp.int32, (all_rows, LANES), 1)
    out_row = row_base - half + lax.broadcasted_iota(jnp.int32, (rows, LANES), 0)
    y = (2 * out_row + 1).astype(jnp.float32) / band_rows - 1.0
    lane = lax.broadcasted_iota(jnp.int32, (rows, LANES), 1)
    cols = [col_base - half + block * step + lane for block in range(blocks)]

    def match(e):
        @pl.when(last_first)
        def _():
            after = slice(2 * tile_rows, 3 * tile_rows)
            window[e, after, :] = choose(moves[e], 0, cross[e], window[e, after, :])
            for i in range(2):
                edges[i, e, after, :] = choose(
                    moves[e], 0, cross_edges[i, e], edges[i, e, after, :]
                )

        first, total = start_ref[e], count_ref[e]
        inside = (out_row >= first) & (out_row < first + total)
        weighting = weight_ref[e] * inside.astype(jnp.float32)
        valid = (window_rows >= first) & (window_rows < first + total)
        pieces = [edges[0, e]]
        for tile in range(tile_cols // LANES):
            pieces.append(window[e, :, tile * LANES : (tile + 1) * LANES])
        pieces.append(edges[1, e])
        parts = []
        for tile, piece in enumerate(pieces):
            col = lane_in + (col_base + (tile - 1) * LANES)
            keep = valid & (col >= 0) & (col < band_cols)
            parts.append(jnp.where(keep, piece.astype(jnp.float32), 0.0))
        for block in range(blocks):
            tile, offset = divmod(LANES - 2 * half + block * step, LANES)
            here = parts[tile]
            if offset:
                here = pltpu.roll(here, LANES - offset, 1)
                after = pltpu.roll(parts[tile + 1], LANES - offset, 1)
                here = jnp.where(lane_in < LANES - offset, here, after)
            shifted[block] = here
        for a in range(side):
            piece = jnp.concatenate(
                [shifted[block, lead + a : lead + a + rows, :] for block in range(blocks)], axis=0
            )
            lhs[:, a * LANES : (a + 1) * LANES] = piece.astype(BF16)
        response = jnp.dot(lhs[...], table[...], preferred_element_type=jnp.float32)
        for block in range(blocks):
            x = (2 * cols[block] + 1).astype(jnp.float32) / band_cols - 1.0
            matched = jnp.zeros((rows, LANES), jnp.float32)
            for k in range(kernels):
                p = [poly_ref[e, k, i] for i in range(6)]
                spatial = (p[0] + y * (p[2] + p[5] * y)) + x * ((p[1] + p[4] * y) + p[3] * x)
                matched = matched + spatial * response[
                    block * rows : (block + 1) * rows, k * LANES : (k + 1) * LANES
                ]
            if e == 0:
                sums[block] = weighting * matched
            else:
                sums[block] += weighting * matched
        return weighting

    @pl.when(last_first)
    def _():
        end(2).wait_recv()

    for i in range(2):

        @pl.when(last_first & has[1 - i])
        def _(i=i):
            end(i).wait_recv()

    arrive(0)
    denominator = match(0)
    for e in range(1, members):

        @pl.when(second == 1)
        def _(e=e):
            over(e).wait_recv()
            here = window[e, tile_rows : 2 * tile_rows, :].astype(jnp.float32)
            passed = jnp.full(here.shape, moves[e] - place, jnp.int32)
            chosen = jnp.where(passed > 0, across[e].astype(jnp.float32), here)
            window[e, tile_rows : 2 * tile_rows, :] = chosen.astype(BF16)
            ship(e, (0, 1, 2))

    for e in range(1, members):
        arrive(e)
        denominator = denominator + match(e)

    in_rows = (out_row >= 0) & (out_row < band_rows)
    divisor = jnp.where(in_rows, denominator, 1.0)
    coadds = []
    for block in range(blocks):
        keep = in_rows & (cols[block] >= 0) & (cols[block] < band_cols)
        coadds.append(jnp.where(keep, sums[block] / divisor, 0.0))
    tiles = spread.shape[1] // LANES
    for tile in range(tiles):
        line = jnp.zeros((rows, LANES), jnp.float32)
        for block in range(blocks):
            low = block * step - tile * LANES
            if low + step <= 0 or low >= LANES:
                continue
            rolled = pltpu.roll(coadds[block], low % LANES, 1) if low % LANES else coadds[block]
            line = jnp.where((lane >= low) & (lane < low + step), rolled, line)
        spread[:, tile * LANES : (tile + 1) * LANES] = line

    def ahead(parts, tile, offset):
        if offset == 0:
            return parts[tile]
        lanes = lax.broadcasted_iota(jnp.int32, parts[tile].shape, 1)
        here = pltpu.roll(parts[tile], LANES - offset, 1)
        after = pltpu.roll(parts[tile + 1], LANES - offset, 1)
        return jnp.where(lanes < LANES - offset, here, after)

    out_tiles = tile_cols // LANES
    mine = [
        spread[half : half + tile_rows, i * LANES : (i + 1) * LANES] for i in range(tiles)
    ]
    for i in range(out_tiles):
        coadd_ref[:, i * LANES : (i + 1) * LANES] = ahead(mine, i, half)
    down = []
    for i in range(tiles):
        total = taps_ref[0] * spread[0:tile_rows, i * LANES : (i + 1) * LANES]
        for t in range(1, side):
            total = total + taps_ref[t] * spread[
                t : t + tile_rows, i * LANES : (i + 1) * LANES
            ]
        down.append(total)
    for i in range(out_tiles):
        total = taps_ref[0] * ahead(down, i, 0)
        for t in range(1, side):
            total = total + taps_ref[t] * ahead(down, i, t)
        detect_ref[:, i * LANES : (i + 1) * LANES] = total

    for e in range(1, members):
        for stage in range(2):
            for i in range(2):
                turned(e, stage, i).wait_send()

    @pl.when(second == 0)
    def _():
        for e in range(1, members):
            over(e).wait_send()

    @pl.when(last_first)
    def _():
        over(0).wait_send()

    @pl.when(first_second)
    def _():
        end(2).wait_send()

    for i in range(2):

        @pl.when(first_second & has[i])
        def _(i=i):
            end(i).wait_send()

    for e in range(members):
        each(e, own(e), (0, 1, 2), lambda n, i, src, e=e: parcel(e, n, i, src).wait_send())


def on_device(
    exposures, basis_kernels, poly_coef, exposure_weight, row_start, row_count, filter_taps
):
    members, tile_rows, tile_cols = exposures.shape
    kernels, side = basis_kernels.shape[:2]
    half = side // 2
    band_rows = tile_rows * lax.axis_size("narrow")
    band_cols = tile_cols * lax.axis_size("wide")
    step = LANES - (side - 1)
    blocks = pl.cdiv(tile_cols + 2 * half, step)
    rows = pl.cdiv(tile_rows + 2 * half, SUBLANES) * SUBLANES
    all_rows = 3 * tile_rows
    width = pl.cdiv(tile_cols + 2 * half, LANES) * LANES
    sizes = (members, kernels, side, band_rows, band_cols, tile_rows, tile_cols)
    out = jax.ShapeDtypeStruct((tile_rows, tile_cols), jnp.float32)
    scalars = pl.BlockSpec(memory_space=pltpu.SMEM)
    vmem = pl.BlockSpec(memory_space=pltpu.VMEM)
    dma = pltpu.SemaphoreType.DMA
    return pl.pallas_call(
        functools.partial(whole_kernel, sizes),
        out_shape=(out, out),
        in_specs=[scalars] * 5 + [vmem] * 2,
        out_specs=(vmem,) * 2,
        scratch_shapes=[
            pltpu.VMEM((members, all_rows, tile_cols), BF16),
            pltpu.VMEM((2, members, all_rows, LANES), BF16),
            pltpu.VMEM((members, 2, tile_rows, tile_cols), BF16),
            pltpu.VMEM((members, 2, tile_rows, tile_cols), BF16),
            pltpu.VMEM((members, tile_rows, tile_cols), BF16),
            pltpu.VMEM((members, tile_rows, tile_cols), BF16),
            pltpu.VMEM((2, members, tile_rows, LANES), BF16),
            pltpu.VMEM((members, tile_rows, tile_cols), BF16),
            pltpu.VMEM((side * LANES, kernels * LANES), BF16),
            pltpu.VMEM((blocks, all_rows, LANES), jnp.float32),
            pltpu.VMEM((blocks * rows, side * LANES), BF16),
            pltpu.VMEM((blocks, rows, LANES), jnp.float32),
            pltpu.VMEM((rows, width), jnp.float32),
            dma((4 * members,)),
            dma((4 * members,)),
            dma((members,)),
            dma((members,)),
            dma((3,)),
            dma((3,)),
            dma((9 * members,)),
            dma((9 * members,)),
        ],
        compiler_params=pltpu.CompilerParams(collective_id=0, has_side_effects=True),
        name="whole",
    )(poly_coef, exposure_weight, row_start, row_count, filter_taps, exposures, basis_kernels)


def solution(mesh):
    placed = (P(None, "narrow", "wide"), P(), P(), P(), P(), P(), P())
    return jax.shard_map(
        on_device,
        mesh=mesh,
        in_specs=placed,
        out_specs=(P("narrow", "wide"), P("narrow", "wide")),
        check_vma=False,
    )
```

time: 87.7 us -> 39.5 us (0.45); the launches traced: 86 us -> 39.2 us
  starting transfers between devices: 45 us -> 0 us
  Pallas kernels: 8.5 us -> 35.2 us
  waiting for transfers between devices: 19.6 us -> 0 us
  between operations: 8.53 us -> 0.65 us
  other arithmetic: 1.06 us -> 0 us
    ppermute x9 -> x0, starting transfers between devices: 45 us -> none  [the longest x5 25.5 us: moved(): lax.ppermute(array, 'narrow', [(i, i + shift) for i in range(peers - shif...]
    pallas_call x1, Pallas kernels: 8.5 us -> 35.2 us  [on_device(): pl.pallas_call(functools.partial(whole_kernel, sizes), out_shape=(out, ou...]
    ppermute x9 -> x0, waiting for transfers between devices: 19.6 us -> none  [the longest x2 12.1 us: padded(): lax.ppermute(lax.slice_in_dim(array, 0, width, axis=dim), axis, down)]
    unnamed x7 -> x5, local copies, waits for them, and re-layouts: 0.02 us -> 3.37 us
    slice x4 -> x0, local copies, waits for them, and re-layouts: 1.47 us -> none  [the longest x1 1.36 us: on_device(): shifts = [row_start[e] // tile_rows for e in range(1, members)]]
    concatenate x2 -> x0, other arithmetic: 0.93 us -> none  [the longest x1 0.7 us: on_device(): jnp.concatenate([taps[:, :1], jnp.zeros((kernels * side, step - 1), jnp.f...]
  transfers between devices with their start and end apart: 9 -> 0, of which waited for: 5 -> 0; matrix products, arithmetic and copies ran while one was open for 2% -> 0% of each run, Pallas kernels for 0% -> 0%
where the time goes in v3:
time: 39.5 us; the launch traced here: 39.2 us
  Pallas kernels  35.2 us (89%)
  local copies, waits for them, and re-layouts  3.37 us (9%)
  between operations  0.65 us (2%)
    pallas_call x1, Pallas kernels, on_device(): pl.pallas_call(functools.partial(whole_kernel, sizes), out_shape=(out, ou...  35.2 us
    unnamed x5, local copies, waits for them, and re-layouts  3.37 us

profile of v3, /device:TPU:57, one launch (start us, length us, event | category | flops | bytes accessed | tf_op | source)
XLA Modules:
  0.0 39.2 jit_solution(7795299886526624185)
XLA Ops:
  0.6 1.3 %copy.9.poly_ref = f32[4,5,6]{2,1,0:T(8,128)} copy(f32[4,5,6]{2,0,1:T(4,128)} %param.9) | data formatting | bytes 960 | tf_op args[2]
  1.9 35.2 %whole.1 = (f32[32,384]{1,0:T(8,128)}, f32[32,384]{1,0:T(8,128)}) custom-call(f32[4,5,6]{2,1,0:T(8,128)} %copy.9.poly_ref, f32[4]{0:T(128)} %weight_ref.1, s32[4]{0:T(128)} %start_ref.1, s32[4]{0:T(128)} %count_ref.1, f32[21]{0:T(128)} %taps_ref.1, bf16[4,32,384]{2,1,0:T(8,128)(2,1)} %x_ref.1, bf16[5,21,21]{2,1,0:T(8,128)(2,1)} %basis_ref.1), custom_call_target="tpu_custom_call" | custom-call | tf_op jit(solution)/shard_map/whole/pallas_call | solution.py:434
  37.1 0.0 copy-start
  37.1 1.4 %copy.12 = f32[32,384]{1,0:T(8,128)} copy(f32[32,384]{1,0:T(8,128)} %get-tuple-element.4) | data formatting | bytes 98304
  38.6 0.0 copy-done
  38.6 0.6 %copy.13 = f32[32,384]{1,0:T(8,128)} copy(f32[32,384]{1,0:T(8,128)S(1)} %copy-done) | data formatting | bytes 98304
Async XLA Ops:
  37.1 1.4 %copy-start = (f32[32,384]{1,0:T(8,128)S(1)}, f32[32,384]{1,0:T(8,128)}, u32[]{:S(2)}) copy-start(f32[32,384]{1,0:T(8,128)} %get-tuple-element.5) | copy-start | bytes 147460

commit v4 on v3

--- a/solution.py
+++ b/solution.py
@@ -24,8 +24,7 @@
     taps_ref,
     x_ref,
     basis_ref,
-    coadd_ref,
-    detect_ref,
+    result_ref,
     window,
     edges,
     far,
@@ -94,11 +93,7 @@
             for turn in (1, -1):
                 greet({"narrow": on_ring(turn), "wide": beside})
 
-        @pl.when(has[i] & at_end)
-        def _(beside=beside):
-            greet({"narrow": over_end, "wide": beside})
-
-        count = count + 3 * has[i].astype(jnp.int32) + (has[i] & at_end).astype(jnp.int32)
+        count = count + 3 * has[i].astype(jnp.int32)
 
     tap = lax.broadcasted_iota(jnp.int32, (side, LANES), 0)
     spot = lax.broadcasted_iota(jnp.int32, (side, LANES), 1)
@@ -142,11 +137,11 @@
         if i == 2:
             return copy(x_ref, cross, end_sent.at[2], end_got.at[2], {"narrow": over_end})
         return copy(
-            x_ref.at[:, :, lanes_of(i)],
+            cross.at[:, :, lanes_of(i)],
             cross_edges.at[1 - i],
             end_sent.at[i],
             end_got.at[i],
-            {"narrow": over_end, "wide": column + 2 * i - 1},
+            {"wide": column + 2 * i - 1},
         )
 
     def parcel(e, n, i, src):
@@ -222,12 +217,6 @@
     @pl.when(first_second)
     def _():
         end(2).start()
-
-    for i in range(2):
-
-        @pl.when(first_second & has[i])
-        def _(i=i):
-            end(i).start()
 
     for e in range(1, members):
         for i in range(2):
@@ -302,7 +291,7 @@
             x = (2 * cols[block] + 1).astype(jnp.float32) / band_cols - 1.0
             matched = jnp.zeros((rows, LANES), jnp.float32)
             for k in range(kernels):
-                p = [poly_ref[e, k, i] for i in range(6)]
+                p = [poly_ref[k, e, i] for i in range(6)]
                 spatial = (p[0] + y * (p[2] + p[5] * y)) + x * ((p[1] + p[4] * y) + p[3] * x)
                 matched = matched + spatial * response[
                     block * rows : (block + 1) * rows, k * LANES : (k + 1) * LANES
@@ -316,6 +305,12 @@
     @pl.when(last_first)
     def _():
         end(2).wait_recv()
+
+    for i in range(2):
+
+        @pl.when(last_first & has[i])
+        def _(i=i):
+            end(i).start()
 
     for i in range(2):
 
@@ -370,7 +365,7 @@
         spread[half : half + tile_rows, i * LANES : (i + 1) * LANES] for i in range(tiles)
     ]
     for i in range(out_tiles):
-        coadd_ref[:, i * LANES : (i + 1) * LANES] = ahead(mine, i, half)
+        result_ref[0, :, i * LANES : (i + 1) * LANES] = ahead(mine, i, half)
     down = []
     for i in range(tiles):
         total = taps_ref[0] * spread[0:tile_rows, i * LANES : (i + 1) * LANES]
@@ -383,7 +378,7 @@
         total = taps_ref[0] * ahead(down, i, 0)
         for t in range(1, side):
             total = total + taps_ref[t] * ahead(down, i, t)
-        detect_ref[:, i * LANES : (i + 1) * LANES] = total
+        result_ref[1, :, i * LANES : (i + 1) * LANES] = total
 
     for e in range(1, members):
         for stage in range(2):
@@ -405,7 +400,7 @@
 
     for i in range(2):
 
-        @pl.when(first_second & has[i])
+        @pl.when(last_first & has[i])
         def _(i=i):
             end(i).wait_send()
 
@@ -427,15 +422,15 @@
     all_rows = 3 * tile_rows
     width = pl.cdiv(tile_cols + 2 * half, LANES) * LANES
     sizes = (members, kernels, side, band_rows, band_cols, tile_rows, tile_cols)
-    out = jax.ShapeDtypeStruct((tile_rows, tile_cols), jnp.float32)
+    out = jax.ShapeDtypeStruct((2, tile_rows, tile_cols), jnp.float32)
     scalars = pl.BlockSpec(memory_space=pltpu.SMEM)
     vmem = pl.BlockSpec(memory_space=pltpu.VMEM)
     dma = pltpu.SemaphoreType.DMA
-    return pl.pallas_call(
+    results = pl.pallas_call(
         functools.partial(whole_kernel, sizes),
-        out_shape=(out, out),
+        out_shape=out,
         in_specs=[scalars] * 5 + [vmem] * 2,
-        out_specs=(vmem,) * 2,
+        out_specs=vmem,
         scratch_shapes=[
             pltpu.VMEM((members, all_rows, tile_cols), BF16),
             pltpu.VMEM((2, members, all_rows, LANES), BF16),
@@ -461,7 +456,8 @@
         ],
         compiler_params=pltpu.CompilerParams(collective_id=0, has_side_effects=True),
         name="whole",
-    )(poly_coef, exposure_weight, row_start, row_count, filter_taps, exposures, basis_kernels)
+    )(poly_coef.transpose(1, 0, 2), exposure_weight, row_start, row_count, filter_taps, exposures, basis_kernels)
+    return results[0], results[1]
 
 
 def solution(mesh):

time: 39.5 us -> 37.8 us (0.957)
  local copies, waits for them, and re-layouts: 3.37 us -> 1.46 us
    unnamed x5 -> x0, local copies, waits for them, and re-layouts: 3.37 us -> none
    squeeze x0 -> x1, local copies, waits for them, and re-layouts: none -> 1.46 us  [on_device(): return (results[0], results[1])]
where the time goes in v4:
time: 37.8 us; the launch traced here: 37.4 us
  Pallas kernels  35.3 us (93%)
  local copies, waits for them, and re-layouts  1.46 us (4%)
  between operations  0.64 us (2%)
    pallas_call x1, Pallas kernels, on_device(): pl.pallas_call(functools.partial(whole_kernel, sizes), out_shape=out, in_...  35.3 us
    squeeze x1, local copies, waits for them, and re-layouts, on_device(): return (results[0], results[1])  1.46 us

profile of v4, /device:TPU:57, one launch (start us, length us, event | category | flops | bytes accessed | tf_op | source)
XLA Modules:
  0.0 37.4 jit_solution(10227809892571551421)
XLA Ops:
  0.6 35.3 %whole.1 = f32[2,32,384]{2,1,0:T(8,128)} custom-call(f32[5,4,6]{2,1,0:T(4,128)} %bitcast.5, f32[4]{0:T(128)} %weight_ref.1, s32[4]{0:T(128)} %start_ref.1, s32[4]{0:T(128)} %count_ref.1, f32[21]{0:T(128)} %taps_ref.1, bf16[4,32,384]{2,1,0:T(8,128)(2,1)} %x_ref.1, bf16[5,21,21]{2,1,0:T(8,128)(2,1)} %basis_ref.1), custom_call_target="tpu_custom_call" | custom-call | tf_op jit(solution)/shard_map/whole/pallas_call | solution.py:429
  35.9 1.5 %slice_bitcast_fusion = (f32[32,384]{1,0:T(8,128)}, f32[32,384]{1,0:T(8,128)}) fusion(f32[2,32,384]{2,1,0:T(8,128)} %whole.1), kind=kLoop, calls=%fused_computation | loop fusion | bytes 196608 | tf_op jit(solution)/shard_map/squeeze | solution.py:460

commit v5 on v4

--- a/solution.py
+++ b/solution.py
@@ -22,9 +22,10 @@
     start_ref,
     count_ref,
     taps_ref,
-    x_ref,
+    x_hbm,
     basis_ref,
     result_ref,
+    x_ref,
     window,
     edges,
     far,
@@ -46,6 +47,7 @@
     end_got,
     ship_sent,
     ship_got,
+    fetched,
 ):
     members, kernels, side, band_rows, band_cols, tile_rows, tile_cols = sizes
     half = side // 2
@@ -68,6 +70,8 @@
     other = (1 - second) * ring + place
     over_end = (1 - second) * ring + (ring - 1 - place)
 
+    fetch = pltpu.make_async_copy(x_hbm, x_ref, fetched)
+    fetch.start()
     barrier = pltpu.get_barrier_semaphore()
 
     def greet(peer):
@@ -95,17 +99,7 @@
 
         count = count + 3 * has[i].astype(jnp.int32)
 
-    tap = lax.broadcasted_iota(jnp.int32, (side, LANES), 0)
-    spot = lax.broadcasted_iota(jnp.int32, (side, LANES), 1)
-    reverse = jnp.where((tap + spot == LANES) | (tap + spot == 0), 1.0, 0.0).astype(BF16)
-    for k in range(kernels):
-        seeds = jnp.dot(basis_ref[k], reverse, preferred_element_type=jnp.float32)
-        for a in range(side):
-            seed = jnp.broadcast_to(seeds[a : a + 1, :], (LANES, LANES))
-            band = pltpu.roll(seed, 0, 1, stride=1, stride_axis=0)
-            table[a * LANES : (a + 1) * LANES, k * LANES : (k + 1) * LANES] = band.astype(BF16)
-    window[0, tile_rows : 2 * tile_rows, :] = x_ref[0]
-
+    fetch.wait()
     pl.semaphore_wait(barrier, count)
 
     def copy(src, dst, send_sem, recv_sem, peer):
@@ -204,6 +198,7 @@
         for i in range(2):
             turned(e, 0, i).start()
 
+    window[0, tile_rows : 2 * tile_rows, :] = x_ref[0]
     @pl.when(last_first)
     def _():
         over(0).start()
@@ -217,6 +212,16 @@
     @pl.when(first_second)
     def _():
         end(2).start()
+
+    tap = lax.broadcasted_iota(jnp.int32, (side, LANES), 0)
+    spot = lax.broadcasted_iota(jnp.int32, (side, LANES), 1)
+    reverse = jnp.where((tap + spot == LANES) | (tap + spot == 0), 1.0, 0.0).astype(BF16)
+    for k in range(kernels):
+        seeds = jnp.dot(basis_ref[k], reverse, preferred_element_type=jnp.float32)
+        for a in range(side):
+            seed = jnp.broadcast_to(seeds[a : a + 1, :], (LANES, LANES))
+            band = pltpu.roll(seed, 0, 1, stride=1, stride_axis=0)
+            table[a * LANES : (a + 1) * LANES, k * LANES : (k + 1) * LANES] = band.astype(BF16)
 
     for e in range(1, members):
         for i in range(2):
@@ -300,8 +305,6 @@
                 sums[block] = weighting * matched
             else:
                 sums[block] += weighting * matched
-        return weighting
-
     @pl.when(last_first)
     def _():
         end(2).wait_recv()
@@ -319,7 +322,7 @@
             end(i).wait_recv()
 
     arrive(0)
-    denominator = match(0)
+    match(0)
     for e in range(1, members):
 
         @pl.when(second == 1)
@@ -331,16 +334,21 @@
             window[e, tile_rows : 2 * tile_rows, :] = chosen.astype(BF16)
             ship(e, (0, 1, 2))
 
+    denominator = jnp.zeros((rows, LANES), jnp.float32)
+    for e in range(members):
+        inside = (out_row >= start_ref[e]) & (out_row < start_ref[e] + count_ref[e])
+        denominator = denominator + weight_ref[e] * inside.astype(jnp.float32)
+    in_rows = (out_row >= 0) & (out_row < band_rows)
+    inverse = 1.0 / jnp.where(in_rows, denominator, 1.0)
+
     for e in range(1, members):
         arrive(e)
-        denominator = denominator + match(e)
-
-    in_rows = (out_row >= 0) & (out_row < band_rows)
-    divisor = jnp.where(in_rows, denominator, 1.0)
+        match(e)
+
     coadds = []
     for block in range(blocks):
         keep = in_rows & (cols[block] >= 0) & (cols[block] < band_cols)
-        coadds.append(jnp.where(keep, sums[block] / divisor, 0.0))
+        coadds.append(jnp.where(keep, sums[block] * inverse, 0.0))
     tiles = spread.shape[1] // LANES
     for tile in range(tiles):
         line = jnp.zeros((rows, LANES), jnp.float32)
@@ -374,11 +382,15 @@
                 t : t + tile_rows, i * LANES : (i + 1) * LANES
             ]
         down.append(total)
+    totals = [taps_ref[0] * down[i] for i in range(out_tiles)]
+    lanes = lax.broadcasted_iota(jnp.int32, down[0].shape, 1)
+    for t in range(1, side):
+        rolled = [pltpu.roll(part, LANES - t, 1) for part in down]
+        for i in range(out_tiles):
+            here = jnp.where(lanes < LANES - t, rolled[i], rolled[i + 1])
+            totals[i] = totals[i] + taps_ref[t] * here
     for i in range(out_tiles):
-        total = taps_ref[0] * ahead(down, i, 0)
-        for t in range(1, side):
-            total = total + taps_ref[t] * ahead(down, i, t)
-        result_ref[1, :, i * LANES : (i + 1) * LANES] = total
+        result_ref[1, :, i * LANES : (i + 1) * LANES] = totals[i]
 
     for e in range(1, members):
         for stage in range(2):
@@ -429,9 +441,10 @@
     results = pl.pallas_call(
         functools.partial(whole_kernel, sizes),
         out_shape=out,
-        in_specs=[scalars] * 5 + [vmem] * 2,
+        in_specs=[scalars] * 5 + [pl.BlockSpec(memory_space=pl.ANY), vmem],
         out_specs=vmem,
         scratch_shapes=[
+            pltpu.VMEM((members, tile_rows, tile_cols), BF16),
             pltpu.VMEM((members, all_rows, tile_cols), BF16),
             pltpu.VMEM((2, members, all_rows, LANES), BF16),
             pltpu.VMEM((members, 2, tile_rows, tile_cols), BF16),
@@ -453,6 +466,7 @@
             dma((3,)),
             dma((9 * members,)),
             dma((9 * members,)),
+            dma,
         ],
         compiler_params=pltpu.CompilerParams(collective_id=0, has_side_effects=True),
         name="whole",

time: 37.8 us -> 37.9 us (level)
  no operation moved by 1% of the time
where the time goes in v5:
time: 37.9 us; the launch traced here: 37.4 us
  Pallas kernels  35.3 us (93%)
  local copies, waits for them, and re-layouts  1.46 us (4%)
  between operations  0.64 us (2%)
    pallas_call x1, Pallas kernels, on_device(): pl.pallas_call(functools.partial(whole_kernel, sizes), out_shape=out, in_...  35.3 us
    squeeze x1, local copies, waits for them, and re-layouts, on_device(): return (results[0], results[1])  1.46 us

profile of v5, /device:TPU:57, one launch (start us, length us, event | category | flops | bytes accessed | tf_op | source)
XLA Modules:
  0.0 37.4 jit_solution(4958531051669958719)
XLA Ops:
  0.6 35.3 %whole.1 = f32[2,32,384]{2,1,0:T(8,128)} custom-call(f32[5,4,6]{2,1,0:T(4,128)} %bitcast.5, f32[4]{0:T(128)} %weight_ref.1, s32[4]{0:T(128)} %start_ref.1, s32[4]{0:T(128)} %count_ref.1, f32[21]{0:T(128)} %taps_ref.1, bf16[4,32,384]{2,1,0:T(8,128)(2,1)} %x_hbm.1, bf16[5,21,21]{2,1,0:T(8,128)(2,1)} %basis_ref.1), custom_call_target="tpu_custom_call" | custom-call | tf_op jit(solution)/shard_map/whole/pallas_call | solution.py:441
  35.9 1.5 %slice_bitcast_fusion = (f32[32,384]{1,0:T(8,128)}, f32[32,384]{1,0:T(8,128)}) fusion(f32[2,32,384]{2,1,0:T(8,128)} %whole.1), kind=kLoop, calls=%fused_computation | loop fusion | bytes 196608 | tf_op jit(solution)/shard_map/squeeze | solution.py:474

commit v6 on v5

--- a/solution.py
+++ b/solution.py
@@ -115,14 +115,35 @@
     def own(e):
         return window.at[e, tile_rows : 2 * tile_rows, :]
 
-    def turned(e, stage, i):
+    part = tile_rows // 2
+
+    def rows_of(h):
+        return slice(h * part, (h + 1) * part)
+
+    def own_rows(h):
+        return slice(tile_rows + h * part, tile_rows + (h + 1) * part)
+
+    def turned(e, stage, i, h):
         src, into, by = ((x_ref, far, 3), (held, near, 1))[stage]
-        slot = (2 * e + stage) * 2 + i
+        slot = ((2 * e + stage) * 2 + i) * 2 + h
         peer = {"narrow": on_ring(by - 2 * by * i)}
-        return copy(src.at[e], into.at[e, i], turn_sent.at[slot], turn_got.at[slot], peer)
-
-    def over(e):
-        return copy(own(e), across.at[e], over_sent.at[e], over_got.at[e], {"narrow": other})
+        return copy(
+            src.at[e, rows_of(h)],
+            into.at[e, i, rows_of(h)],
+            turn_sent.at[slot],
+            turn_got.at[slot],
+            peer,
+        )
+
+    def over(e, h):
+        slot = 2 * e + h
+        return copy(
+            window.at[e, own_rows(h), :],
+            across.at[e, rows_of(h)],
+            over_sent.at[slot],
+            over_got.at[slot],
+            {"narrow": other},
+        )
 
     def lanes_of(i):
         return slice(0, LANES) if i == 0 else slice(tile_cols - LANES, tile_cols)
@@ -195,13 +216,15 @@
     low = [t - 3 * h for t, h in zip(turns, high)]
 
     for e in range(1, members):
-        for i in range(2):
-            turned(e, 0, i).start()
+        for h in range(2):
+            for i in range(2):
+                turned(e, 0, i, h).start()
 
     window[0, tile_rows : 2 * tile_rows, :] = x_ref[0]
     @pl.when(last_first)
     def _():
-        over(0).start()
+        for h in range(2):
+            over(0, h).start()
 
     ship(0, (1, 2))
 
@@ -223,29 +246,43 @@
             band = pltpu.roll(seed, 0, 1, stride=1, stride_axis=0)
             table[a * LANES : (a + 1) * LANES, k * LANES : (k + 1) * LANES] = band.astype(BF16)
 
-    for e in range(1, members):
+    def turn_high(e, h):
         for i in range(2):
-            turned(e, 0, i).wait_recv()
-        held[e] = choose(high[e], 1, far[e, 0], choose(high[e], -1, far[e, 1], x_ref[e]))
+            turned(e, 0, i, h).wait_recv()
+        at = rows_of(h)
+        held[e, at] = choose(
+            high[e], 1, far[e, 0, at], choose(high[e], -1, far[e, 1, at], x_ref[e, at])
+        )
         for i in range(2):
-            turned(e, 1, i).start()
+            turned(e, 1, i, h).start()
+
+    def turn_low(e, h):
+        for i in range(2):
+            turned(e, 1, i, h).wait_recv()
+        at = rows_of(h)
+        window[e, own_rows(h), :] = choose(
+            low[e], 1, near[e, 0, at], choose(low[e], -1, near[e, 1, at], held[e, at])
+        )
+
+        @pl.when(second == 0)
+        def _():
+            over(e, h).start()
+            if h == 1:
+                ship(e, (0, 1, 2))
+
+    halves = [(e, h) for e in range(1, members) for h in range(2)]
+    lag = 3
+    for j in range(len(halves) + lag):
+        if j < len(halves):
+            turn_high(*halves[j])
+        if j >= lag:
+            turn_low(*halves[j - lag])
 
     @pl.when(last_second)
     def _():
-        over(0).wait_recv()
+        for h in range(2):
+            over(0, h).wait_recv()
         each(0, across.at[0], (0,), lambda n, i, src: parcel(0, n, i, src).start())
-
-    for e in range(1, members):
-        for i in range(2):
-            turned(e, 1, i).wait_recv()
-        window[e, tile_rows : 2 * tile_rows, :] = choose(
-            low[e], 1, near[e, 0], choose(low[e], -1, near[e, 1], held[e])
-        )
-
-        @pl.when(second == 0)
-        def _(e=e):
-            over(e).start()
-            ship(e, (0, 1, 2))
 
     all_rows, lead = shifted.shape[1], tile_rows - 2 * half
     window_rows = row_base - tile_rows + lax.broadcasted_iota(jnp.int32, (all_rows, LANES), 0)
@@ -327,7 +364,8 @@
 
         @pl.when(second == 1)
         def _(e=e):
-            over(e).wait_recv()
+            for h in range(2):
+                over(e, h).wait_recv()
             here = window[e, tile_rows : 2 * tile_rows, :].astype(jnp.float32)
             passed = jnp.full(here.shape, moves[e] - place, jnp.int32)
             chosen = jnp.where(passed > 0, across[e].astype(jnp.float32), here)
@@ -395,16 +433,19 @@
     for e in range(1, members):
         for stage in range(2):
             for i in range(2):
-                turned(e, stage, i).wait_send()
+                for h in range(2):
+                    turned(e, stage, i, h).wait_send()
 
     @pl.when(second == 0)
     def _():
         for e in range(1, members):
-            over(e).wait_send()
+            for h in range(2):
+                over(e, h).wait_send()
 
     @pl.when(last_first)
     def _():
-        over(0).wait_send()
+        for h in range(2):
+            over(0, h).wait_send()
 
     @pl.when(first_second)
     def _():
@@ -458,10 +499,10 @@
             pltpu.VMEM((blocks * rows, side * LANES), BF16),
             pltpu.VMEM((blocks, rows, LANES), jnp.float32),
             pltpu.VMEM((rows, width), jnp.float32),
-            dma((4 * members,)),
-            dma((4 * members,)),
-            dma((members,)),
-            dma((members,)),
+            dma((8 * members,)),
+            dma((8 * members,)),
+            dma((2 * members,)),
+            dma((2 * members,)),
             dma((3,)),
             dma((3,)),
             dma((9 * members,)),

time: 37.9 us -> 38.6 us (1.018)
  the two profiles are of different devices: /device:TPU:57 before, /device:TPU:456 now
where the time goes in v6:
time: 38.6 us; the launch traced here: 38.3 us
  Pallas kernels  36.2 us (94%)
  local copies, waits for them, and re-layouts  1.46 us (4%)
  between operations  0.64 us (2%)
    pallas_call x1, Pallas kernels, on_device(): pl.pallas_call(functools.partial(whole_kernel, sizes), out_shape=out, in_...  36.2 us
    squeeze x1, local copies, waits for them, and re-layouts, on_device(): return (results[0], results[1])  1.46 us

profile of v6, /device:TPU:456, one launch (start us, length us, event | category | flops | bytes accessed | tf_op | source)
XLA Modules:
  0.0 38.3 jit_solution(16436159739386892884)
XLA Ops:
  0.6 36.2 %whole.1 = f32[2,32,384]{2,1,0:T(8,128)} custom-call(f32[5,4,6]{2,1,0:T(4,128)} %bitcast.5, f32[4]{0:T(128)} %weight_ref.1, s32[4]{0:T(128)} %start_ref.1, s32[4]{0:T(128)} %count_ref.1, f32[21]{0:T(128)} %taps_ref.1, bf16[4,32,384]{2,1,0:T(8,128)(2,1)} %x_hbm.1, bf16[5,21,21]{2,1,0:T(8,128)(2,1)} %basis_ref.1), custom_call_target="tpu_custom_call" | custom-call | tf_op jit(solution)/shard_map/whole/pallas_call | solution.py:482
  36.8 1.5 %slice_bitcast_fusion = (f32[32,384]{1,0:T(8,128)}, f32[32,384]{1,0:T(8,128)}) fusion(f32[2,32,384]{2,1,0:T(8,128)} %whole.1), kind=kLoop, calls=%fused_computation | loop fusion | bytes 196608 | tf_op jit(solution)/shard_map/squeeze | solution.py:515

commit v7 on v5

--- a/solution.py
+++ b/solution.py
@@ -360,37 +360,13 @@
             line = jnp.where((lane >= low) & (lane < low + step), rolled, line)
         spread[:, tile * LANES : (tile + 1) * LANES] = line
 
-    def ahead(parts, tile, offset):
-        if offset == 0:
-            return parts[tile]
-        lanes = lax.broadcasted_iota(jnp.int32, parts[tile].shape, 1)
-        here = pltpu.roll(parts[tile], LANES - offset, 1)
-        after = pltpu.roll(parts[tile + 1], LANES - offset, 1)
-        return jnp.where(lanes < LANES - offset, here, after)
-
-    out_tiles = tile_cols // LANES
-    mine = [
-        spread[half : half + tile_rows, i * LANES : (i + 1) * LANES] for i in range(tiles)
-    ]
-    for i in range(out_tiles):
-        result_ref[0, :, i * LANES : (i + 1) * LANES] = ahead(mine, i, half)
-    down = []
     for i in range(tiles):
-        total = taps_ref[0] * spread[0:tile_rows, i * LANES : (i + 1) * LANES]
+        at = slice(i * LANES, (i + 1) * LANES)
+        result_ref[0, :, at] = spread[half : half + tile_rows, at]
+        total = taps_ref[0] * spread[0:tile_rows, at]
         for t in range(1, side):
-            total = total + taps_ref[t] * spread[
-                t : t + tile_rows, i * LANES : (i + 1) * LANES
-            ]
-        down.append(total)
-    totals = [taps_ref[0] * down[i] for i in range(out_tiles)]
-    lanes = lax.broadcasted_iota(jnp.int32, down[0].shape, 1)
-    for t in range(1, side):
-        rolled = [pltpu.roll(part, LANES - t, 1) for part in down]
-        for i in range(out_tiles):
-            here = jnp.where(lanes < LANES - t, rolled[i], rolled[i + 1])
-            totals[i] = totals[i] + taps_ref[t] * here
-    for i in range(out_tiles):
-        result_ref[1, :, i * LANES : (i + 1) * LANES] = totals[i]
+            total = total + taps_ref[t] * spread[t : t + tile_rows, at]
+        result_ref[1, :, at] = total
 
     for e in range(1, members):
         for stage in range(2):
@@ -418,6 +394,27 @@
 
     for e in range(members):
         each(e, own(e), (0, 1, 2), lambda n, i, src, e=e: parcel(e, n, i, src).wait_send())
+
+
+def across_kernel(side, taps_ref, rows_ref, coadd_ref, detect_ref):
+    half = side // 2
+    tiles = rows_ref.shape[2] // LANES
+    own, down = [
+        [rows_ref[n, :, i * LANES : (i + 1) * LANES] for i in range(tiles)] for n in range(2)
+    ]
+    lanes = lax.broadcasted_iota(jnp.int32, down[0].shape, 1)
+
+    def ahead(parts, t):
+        rolled = [pltpu.roll(part, LANES - t, 1) for part in parts]
+        return [jnp.where(lanes < LANES - t, a, b) for a, b in zip(rolled, rolled[1:])]
+
+    for i, value in enumerate(ahead(own, half)):
+        coadd_ref[:, i * LANES : (i + 1) * LANES] = value
+    totals = [taps_ref[0] * part for part in down[:-1]]
+    for t in range(1, side):
+        totals = [total + taps_ref[t] * value for total, value in zip(totals, ahead(down, t))]
+    for i, total in enumerate(totals):
+        detect_ref[:, i * LANES : (i + 1) * LANES] = total
 
 
 def on_device(
@@ -434,13 +431,13 @@
     all_rows = 3 * tile_rows
     width = pl.cdiv(tile_cols + 2 * half, LANES) * LANES
     sizes = (members, kernels, side, band_rows, band_cols, tile_rows, tile_cols)
-    out = jax.ShapeDtypeStruct((2, tile_rows, tile_cols), jnp.float32)
+    out = jax.ShapeDtypeStruct((tile_rows, tile_cols), jnp.float32)
     scalars = pl.BlockSpec(memory_space=pltpu.SMEM)
     vmem = pl.BlockSpec(memory_space=pltpu.VMEM)
     dma = pltpu.SemaphoreType.DMA
     results = pl.pallas_call(
         functools.partial(whole_kernel, sizes),
-        out_shape=out,
+        out_shape=jax.ShapeDtypeStruct((2, tile_rows, width), jnp.float32),
         in_specs=[scalars] * 5 + [pl.BlockSpec(memory_space=pl.ANY), vmem],
         out_specs=vmem,
         scratch_shapes=[
@@ -471,7 +468,13 @@
         compiler_params=pltpu.CompilerParams(collective_id=0, has_side_effects=True),
         name="whole",
     )(poly_coef.transpose(1, 0, 2), exposure_weight, row_start, row_count, filter_taps, exposures, basis_kernels)
-    return results[0], results[1]
+    return pl.pallas_call(
+        functools.partial(across_kernel, side),
+        out_shape=(out, out),
+        in_specs=[scalars, vmem],
+        out_specs=(vmem,) * 2,
+        name="across",
+    )(filter_taps, results)
 
 
 def solution(mesh):

time: 37.9 us -> 38.1 us (level)
  Pallas kernels: 35.3 us -> 37 us
  local copies, waits for them, and re-layouts: 1.46 us -> 0 us
    pallas_call x1 -> x2, Pallas kernels: 35.3 us -> 37 us  [the longest x1 35 us: on_device(): pl.pallas_call(functools.partial(whole_kernel, sizes), out_shape=jax.Shap...]
    squeeze x1 -> x0, local copies, waits for them, and re-layouts: 1.46 us -> none  [on_device(): return (results[0], results[1])]
where the time goes in v7:
time: 38.1 us; the launch traced here: 37.6 us
  Pallas kernels  37 us (97%)
  between operations  0.64 us (2%)
    pallas_call x1, Pallas kernels, on_device(): pl.pallas_call(functools.partial(whole_kernel, sizes), out_shape=jax.Shap...  35 us
    pallas_call x1, Pallas kernels, on_device(): pl.pallas_call(functools.partial(across_kernel, side), out_shape=(out, ou...  1.96 us

profile of v7, /device:TPU:57, one launch (start us, length us, event | category | flops | bytes accessed | tf_op | source)
XLA Modules:
  0.0 37.6 jit_solution(16100167022400235347)
XLA Ops:
  0.6 35.0 %whole.1.rows_ref = f32[2,32,512]{2,1,0:T(8,128)} custom-call(f32[5,4,6]{2,1,0:T(4,128)} %bitcast.1, f32[4]{0:T(128)} %weight_ref.1, s32[4]{0:T(128)} %start_ref.1, s32[4]{0:T(128)} %count_ref.1, f32[21]{0:T(128)} %taps_ref.3, bf16[4,32,384]{2,1,0:T(8,128)(2,1)} %x_hbm.1, bf16[5,21,21]{2,1,0:T(8,128)(2,1)} %basis_ref.1), custom_call_target="tpu_custom_call" | custom-call | tf_op jit(solution)/shard_map/whole/pallas_call | solution.py:438
  35.6 2.0 %across.1 = (f32[32,384]{1,0:T(8,128)}, f32[32,384]{1,0:T(8,128)}) custom-call(f32[21]{0:T(128)} %taps_ref.3, f32[2,32,512]{2,1,0:T(8,128)} %whole.1.rows_ref), custom_call_target="tpu_custom_call" | custom-call | tf_op jit(solution)/shard_map/across/pallas_call | solution.py:471

commit v8 on v5

--- a/solution.py
+++ b/solution.py
@@ -305,24 +305,6 @@
                 sums[block] = weighting * matched
             else:
                 sums[block] += weighting * matched
-    @pl.when(last_first)
-    def _():
-        end(2).wait_recv()
-
-    for i in range(2):
-
-        @pl.when(last_first & has[i])
-        def _(i=i):
-            end(i).start()
-
-    for i in range(2):
-
-        @pl.when(last_first & has[1 - i])
-        def _(i=i):
-            end(i).wait_recv()
-
-    arrive(0)
-    match(0)
     for e in range(1, members):
 
         @pl.when(second == 1)
@@ -334,6 +316,24 @@
             window[e, tile_rows : 2 * tile_rows, :] = chosen.astype(BF16)
             ship(e, (0, 1, 2))
 
+    @pl.when(last_first)
+    def _():
+        end(2).wait_recv()
+
+    for i in range(2):
+
+        @pl.when(last_first & has[i])
+        def _(i=i):
+            end(i).start()
+
+    for i in range(2):
+
+        @pl.when(last_first & has[1 - i])
+        def _(i=i):
+            end(i).wait_recv()
+
+    arrive(0)
+    match(0)
     denominator = jnp.zeros((rows, LANES), jnp.float32)
     for e in range(members):
         inside = (out_row >= start_ref[e]) & (out_row < start_ref[e] + count_ref[e])

time: 37.9 us -> 37.9 us (level)
  no operation moved by 1% of the time
where the time goes in v8:
time: 37.9 us; the launch traced here: 37.4 us
  Pallas kernels  35.3 us (93%)
  local copies, waits for them, and re-layouts  1.46 us (4%)
  between operations  0.64 us (2%)
    pallas_call x1, Pallas kernels, on_device(): pl.pallas_call(functools.partial(whole_kernel, sizes), out_shape=out, in_...  35.3 us
    squeeze x1, local copies, waits for them, and re-layouts, on_device(): return (results[0], results[1])  1.46 us

profile of v8, /device:TPU:57, one launch (start us, length us, event | category | flops | bytes accessed | tf_op | source)
XLA Modules:
  0.0 37.4 jit_solution(8819636152004582565)
XLA Ops:
  0.6 35.3 %whole.1 = f32[2,32,384]{2,1,0:T(8,128)} custom-call(f32[5,4,6]{2,1,0:T(4,128)} %bitcast.5, f32[4]{0:T(128)} %weight_ref.1, s32[4]{0:T(128)} %start_ref.1, s32[4]{0:T(128)} %count_ref.1, f32[21]{0:T(128)} %taps_ref.1, bf16[4,32,384]{2,1,0:T(8,128)(2,1)} %x_hbm.1, bf16[5,21,21]{2,1,0:T(8,128)(2,1)} %basis_ref.1), custom_call_target="tpu_custom_call" | custom-call | tf_op jit(solution)/shard_map/whole/pallas_call | solution.py:441
  35.9 1.5 %slice_bitcast_fusion = (f32[32,384]{1,0:T(8,128)}, f32[32,384]{1,0:T(8,128)}) fusion(f32[2,32,384]{2,1,0:T(8,128)} %whole.1), kind=kLoop, calls=%fused_computation | loop fusion | bytes 196608 | tf_op jit(solution)/shard_map/squeeze | solution.py:474
